TPU v7x, 32 devices: a whole 2x2x4 slice. The times are simulated.
32 devices in a mesh: dp: 8 (over y, x, core), ctx: 4 (over z).
Axes of the slice: x: 2, y: 2, z: 4, core: 2. Of those that a mesh axis runs over, the one named last changes fastest.
Arguments:
- layer_input: bfloat16 [8, 1024, 1024], P('dp', 'ctx'), may hold values from -6 to 6
- prefix: int32 [8], P('dp'), may hold values from 102 to 512, as said below
- ln1_gain: bfloat16 [1024], P(('dp', 'ctx')), may hold values from 0.5 to 1.5
- ln1_bias: bfloat16 [1024], P(('dp', 'ctx')), may hold values from -3 to 3
- w_qkv: bfloat16 [1024, 3072], P(('dp', 'ctx')), may hold values from -0.1875 to 0.1875
- b_qv: bfloat16 [2048], P(('dp', 'ctx')), may hold values from -4 to 4
- w_out: bfloat16 [1024, 1024], P(('dp', 'ctx')), may hold values from -3 to 3
- b_out: bfloat16 [1024], P(('dp', 'ctx')), may hold values from -3 to 3
- ln2_gain: bfloat16 [1024], P(('dp', 'ctx')), may hold values from 0.5 to 1.5
- ln2_bias: bfloat16 [1024], P(('dp', 'ctx')), may hold values from -3 to 3
- w_up: bfloat16 [1024, 4096], P(('dp', 'ctx')), may hold values from -0.1875 to 0.1875
- b_up: bfloat16 [4096], P(('dp', 'ctx')), may hold values from -4 to 4
- w_down: bfloat16 [4096, 1024], P(('dp', 'ctx')), may hold values from -0.09375 to 0.09375
- b_down: bfloat16 [1024], P(('dp', 'ctx')), may hold values from -6 to 6
- cotangent: bfloat16 [8, 1024, 1024], P('dp', 'ctx'), may hold values from -6 to 6
Outputs:
- layer_out: bfloat16 [8, 1024, 1024], P('dp', 'ctx')
- input_grad: float32 [8, 1024, 1024], P('dp', 'ctx')
- grad_ln1_gain: float32 [1024], P(('dp', 'ctx'))
- grad_ln1_bias: float32 [1024], P(('dp', 'ctx'))
- grad_w_qkv: float32 [1024, 3072], P(('dp', 'ctx'))
- grad_b_qv: float32 [2048], P(('dp', 'ctx'))
- grad_w_out: float32 [1024, 1024], P(('dp', 'ctx'))
- grad_b_out: float32 [1024], P(('dp', 'ctx'))
- grad_ln2_gain: float32 [1024], P(('dp', 'ctx'))
- grad_ln2_bias: float32 [1024], P(('dp', 'ctx'))
- grad_w_up: float32 [1024, 4096], P(('dp', 'ctx'))
- grad_b_up: float32 [4096], P(('dp', 'ctx'))
- grad_w_down: float32 [4096, 1024], P(('dp', 'ctx'))
- grad_b_down: float32 [1024], P(('dp', 'ctx'))
Inputs may be any that keep to these rules, and one draw needn't show every extreme that they name: prefix[s] counts the leading positions of sequence s that attend to one another in both directions; the largest and the smallest allowed values both occur.
All inputs are finite; a program needn't handle non-finite values.
Results may differ from a plain program's by a relative error of at most 0.012.
Values may be sent and summed in bfloat16 or wider, within the bound.
No kernel may reach another device: no remote copies, remote signals or barrier semaphores. Data moves between devices by JAX's collectives and lax.ppermute only.
A program may use at most 192 MiB of HBM per device.

v0:
```python
import jax
import jax.numpy as jnp
from jax import lax
from jax.sharding import PartitionSpec as P

D = 1024
H = 16
HD = 64


NEGATIVE = -1e30


def layer_norm(values, gain, shift):
    center = jnp.mean(values, axis=-1, keepdims=True)
    offsets = values - center
    spread = jnp.mean(offsets * offsets, axis=-1, keepdims=True)
    return offsets * lax.rsqrt(spread + 1e-05) * gain + shift


def gelu_tanh(values):
    return jax.nn.gelu(values, approximate=True)


def masked_scores(query_heads, query_pos, key_heads, key_pos, prefix_len):
    raw_scores = (
        jnp.einsum("qhd,khd->hqk", query_heads, key_heads, preferred_element_type=jnp.float32)
        * 0.125
    )
    allowed = (key_pos[None, :] <= query_pos[:, None]) | (key_pos[None, :] < prefix_len)
    return (jnp.where(allowed[None], raw_scores, NEGATIVE), allowed)


def softmax_rows(query_heads, query_pos, key_heads, key_pos, prefix_len, log_total):
    scores, allowed = masked_scores(query_heads, query_pos, key_heads, key_pos, prefix_len)
    return jnp.where(allowed[None], jnp.exp(scores - log_total[:, :, None]), 0.0)


def per_device(
    layer_input,
    prefix,
    ln1_gain,
    ln1_bias,
    w_qkv,
    b_qv,
    w_out,
    b_out,
    ln2_gain,
    ln2_bias,
    w_up,
    b_up,
    w_down,
    b_down,
    cotangent,
):
    (
        gain_first,
        shift_first,
        proj_qkv,
        bias_qv,
        proj_out,
        bias_out,
        gain_second,
        shift_second,
        proj_up,
        bias_up,
        proj_down,
        bias_down,
    ) = (
        lax.all_gather(ln1_gain, ("dp", "ctx"), axis=0, tiled=True),
        lax.all_gather(ln1_bias, ("dp", "ctx"), axis=0, tiled=True),
        lax.all_gather(w_qkv, ("dp", "ctx"), axis=0, tiled=True),
        lax.all_gather(b_qv, ("dp", "ctx"), axis=0, tiled=True),
        lax.all_gather(w_out, ("dp", "ctx"), axis=0, tiled=True),
        lax.all_gather(b_out, ("dp", "ctx"), axis=0, tiled=True),
        lax.all_gather(ln2_gain, ("dp", "ctx"), axis=0, tiled=True),
        lax.all_gather(ln2_bias, ("dp", "ctx"), axis=0, tiled=True),
        lax.all_gather(w_up, ("dp", "ctx"), axis=0, tiled=True),
        lax.all_gather(b_up, ("dp", "ctx"), axis=0, tiled=True),
        lax.all_gather(w_down, ("dp", "ctx"), axis=0, tiled=True),
        lax.all_gather(b_down, ("dp", "ctx"), axis=0, tiled=True),
    )
    tokens = layer_input.shape[1]
    length = tokens * lax.axis_size("ctx")
    block_rows = min(512, length)
    block_count = length // block_rows
    prefix_len = prefix[0]
    query_pos = lax.axis_index("ctx") * tokens + jnp.arange(tokens, dtype=jnp.int32)
    block_starts = jnp.arange(block_count, dtype=jnp.int32) * block_rows
    local_rows = jnp.arange(block_rows, dtype=jnp.int32)
    inputs = layer_input[0].astype(jnp.float32)
    upstream = cotangent[0].astype(jnp.float32)
    shift_one = shift_first.astype(jnp.float32)
    shift_two = shift_second.astype(jnp.float32)
    hidden_first = layer_norm(inputs, gain_first.astype(jnp.float32), shift_one).astype(
        jnp.bfloat16
    )
    mixed = jnp.dot(hidden_first, proj_qkv, preferred_element_type=jnp.float32)
    bias_pair = bias_qv.astype(jnp.float32)
    queries = (mixed[:, :D] + bias_pair[:D]).astype(jnp.bfloat16)
    keys_own = mixed[:, D : 2 * D].astype(jnp.bfloat16)
    values_own = (mixed[:, 2 * D :] + bias_pair[D:]).astype(jnp.bfloat16)
    keys_all, values_all = (
        lax.all_gather(keys_own, "ctx", axis=0, tiled=True),
        lax.all_gather(values_own, "ctx", axis=0, tiled=True),
    )
    query_heads = queries.reshape(tokens, H, HD)
    key_blocks = keys_all.reshape(block_count, block_rows, H, HD)
    value_blocks = values_all.reshape(block_count, block_rows, H, HD)

    def max_step(state_pair, element):
        key_block, block_start = element
        scores, allowed = masked_scores(
            query_heads, query_pos, key_block, block_start + local_rows, prefix_len
        )
        row_max = jnp.maximum(state_pair[0], jnp.max(scores, axis=-1))
        terms = jnp.where(allowed[None], jnp.exp(scores - row_max[:, :, None]), 0.0)
        row_total = state_pair[1] * jnp.exp(state_pair[0] - row_max) + jnp.sum(terms, axis=-1)
        return ((row_max, row_total), None)

    start_state = (
        jnp.full((H, tokens), NEGATIVE, jnp.float32),
        jnp.zeros((H, tokens), jnp.float32),
    )
    (row_max, row_total), unused = lax.scan(max_step, start_state, (key_blocks, block_starts))
    log_total = row_max + jnp.log(row_total)

    def value_step(attended_sum, element):
        key_block, block_start, value_block = element
        weights_soft = softmax_rows(
            query_heads, query_pos, key_block, block_start + local_rows, prefix_len, log_total
        ).astype(jnp.bfloat16)
        return (
            attended_sum
            + jnp.einsum(
                "hqk,khd->qhd", weights_soft, value_block, preferred_element_type=jnp.float32
            ),
            None,
        )

    attended, unused = lax.scan(
        value_step,
        jnp.zeros((tokens, H, HD), jnp.float32),
        (key_blocks, block_starts, value_blocks),
    )
    attended_low = attended.reshape(tokens, D).astype(jnp.bfloat16)
    branch_one = jnp.dot(
        attended_low, proj_out, preferred_element_type=jnp.float32
    ) + bias_out.astype(jnp.float32)
    resid = inputs + branch_one
    hidden_second = layer_norm(resid, gain_second.astype(jnp.float32), shift_two).astype(
        jnp.bfloat16
    )
    pre_act = jnp.dot(hidden_second, proj_up, preferred_element_type=jnp.float32) + bias_up.astype(
        jnp.float32
    )
    activ = gelu_tanh(pre_act).astype(jnp.bfloat16)
    branch_two = jnp.dot(activ, proj_down, preferred_element_type=jnp.float32) + bias_down.astype(
        jnp.float32
    )
    layer_out = (resid + branch_two).astype(jnp.bfloat16)
    gain_first, proj_qkv, proj_out, gain_second, proj_up, proj_down = (
        lax.all_gather(ln1_gain, ("dp", "ctx"), axis=0, tiled=True),
        lax.all_gather(w_qkv, ("dp", "ctx"), axis=0, tiled=True),
        lax.all_gather(w_out, ("dp", "ctx"), axis=0, tiled=True),
        lax.all_gather(ln2_gain, ("dp", "ctx"), axis=0, tiled=True),
        lax.all_gather(w_up, ("dp", "ctx"), axis=0, tiled=True),
        lax.all_gather(w_down, ("dp", "ctx"), axis=0, tiled=True),
    )
    grad_branch_two = upstream.astype(jnp.bfloat16)
    grad_proj_down = jnp.einsum(
        "tf,td->fd", activ, grad_branch_two, preferred_element_type=jnp.float32
    )
    grad_bias_down = jnp.sum(grad_branch_two.astype(jnp.float32), axis=0)
    grad_activ = jnp.einsum(
        "td,fd->tf", grad_branch_two, proj_down, preferred_element_type=jnp.float32
    )
    gelu_value, gelu_pull = jax.vjp(gelu_tanh, pre_act)
    grad_pre = gelu_pull(grad_activ)[0].astype(jnp.bfloat16)
    grad_proj_up = jnp.einsum(
        "td,tf->df", hidden_second, grad_pre, preferred_element_type=jnp.float32
    )
    grad_bias_up = jnp.sum(grad_pre.astype(jnp.float32), axis=0)
    grad_hidden_second = jnp.einsum(
        "tf,df->td", grad_pre, proj_up, preferred_element_type=jnp.float32
    )
    norm_value, norm_pull = jax.vjp(layer_norm, resid, gain_second.astype(jnp.float32), shift_two)
    resid_part, grad_gain_second, grad_shift_second = norm_pull(grad_hidden_second)
    grad_resid = upstream + resid_part
    grad_branch_one = grad_resid.astype(jnp.bfloat16)
    grad_proj_out = jnp.einsum(
        "td,te->de", attended_low, grad_branch_one, preferred_element_type=jnp.float32
    )
    grad_bias_out = jnp.sum(grad_branch_one.astype(jnp.float32), axis=0)
    grad_attended = jnp.einsum(
        "te,de->td", grad_branch_one, proj_out, preferred_element_type=jnp.float32
    ).astype(jnp.bfloat16)
    grad_heads = grad_attended.reshape(tokens, H, HD)
    row_delta = jnp.sum(grad_heads.astype(jnp.float32) * attended, axis=-1).T

    def back_step(query_sum, element):
        key_block, block_start, value_block = element
        weights_soft = softmax_rows(
            query_heads, query_pos, key_block, block_start + local_rows, prefix_len, log_total
        )
        value_grad = jnp.einsum(
            "hqk,qhd->khd",
            weights_soft.astype(jnp.bfloat16),
            grad_heads,
            preferred_element_type=jnp.float32,
        )
        weight_grad = jnp.einsum(
            "qhd,khd->hqk", grad_heads, value_block, preferred_element_type=jnp.float32
        )
        score_grad = (weights_soft * (weight_grad - row_delta[:, :, None])).astype(jnp.bfloat16)
        query_sum = (
            query_sum
            + jnp.einsum("hqk,khd->qhd", score_grad, key_block, preferred_element_type=jnp.float32)
            * 0.125
        )
        key_grad = (
            jnp.einsum("hqk,qhd->khd", score_grad, query_heads, preferred_element_type=jnp.float32)
            * 0.125
        )
        return (query_sum, (key_grad.reshape(block_rows, D), value_grad.reshape(block_rows, D)))

    query_sum, (key_terms, value_terms) = lax.scan(
        back_step, jnp.zeros((tokens, H, HD), jnp.float32), (key_blocks, block_starts, value_blocks)
    )
    key_sum, value_sum = (
        lax.psum_scatter(
            key_terms.reshape(length, D).astype(jnp.bfloat16),
            "ctx",
            scatter_dimension=0,
            tiled=True,
        ).astype(jnp.float32),
        lax.psum_scatter(
            value_terms.reshape(length, D).astype(jnp.bfloat16),
            "ctx",
            scatter_dimension=0,
            tiled=True,
        ).astype(jnp.float32),
    )
    query_low = query_sum.reshape(tokens, D).astype(jnp.bfloat16)
    key_low = key_sum.astype(jnp.bfloat16)
    value_low = value_sum.astype(jnp.bfloat16)
    grad_qkv = jnp.concatenate([query_low, key_low, value_low], axis=1)
    grad_proj_qkv = jnp.einsum(
        "td,te->de", hidden_first, grad_qkv, preferred_element_type=jnp.float32
    )
    grad_bias_qv = jnp.concatenate(
        [
            jnp.sum(query_low.astype(jnp.float32), axis=0),
            jnp.sum(value_low.astype(jnp.float32), axis=0),
        ]
    )
    grad_hidden_first = jnp.einsum(
        "te,de->td", grad_qkv, proj_qkv, preferred_element_type=jnp.float32
    )
    first_value, first_pull = jax.vjp(layer_norm, inputs, gain_first.astype(jnp.float32), shift_one)
    input_part, grad_gain_first, grad_shift_first = first_pull(grad_hidden_first)
    input_grad = grad_resid + input_part
    (
        sum_gain_first,
        sum_shift_first,
        sum_qkv,
        sum_bias_qv,
        sum_out,
        sum_bias_out,
        sum_gain_second,
        sum_shift_second,
        sum_up,
        sum_bias_up,
        sum_down,
        sum_bias_down,
    ) = (
        lax.psum_scatter(grad_gain_first, ("dp", "ctx"), scatter_dimension=0, tiled=True),
        lax.psum_scatter(grad_shift_first, ("dp", "ctx"), scatter_dimension=0, tiled=True),
        lax.psum_scatter(grad_proj_qkv, ("dp", "ctx"), scatter_dimension=0, tiled=True),
        lax.psum_scatter(grad_bias_qv, ("dp", "ctx"), scatter_dimension=0, tiled=True),
        lax.psum_scatter(grad_proj_out, ("dp", "ctx"), scatter_dimension=0, tiled=True),
        lax.psum_scatter(grad_bias_out, ("dp", "ctx"), scatter_dimension=0, tiled=True),
        lax.psum_scatter(grad_gain_second, ("dp", "ctx"), scatter_dimension=0, tiled=True),
        lax.psum_scatter(grad_shift_second, ("dp", "ctx"), scatter_dimension=0, tiled=True),
        lax.psum_scatter(grad_proj_up, ("dp", "ctx"), scatter_dimension=0, tiled=True),
        lax.psum_scatter(grad_bias_up, ("dp", "ctx"), scatter_dimension=0, tiled=True),
        lax.psum_scatter(grad_proj_down, ("dp", "ctx"), scatter_dimension=0, tiled=True),
        lax.psum_scatter(grad_bias_down, ("dp", "ctx"), scatter_dimension=0, tiled=True),
    )
    return (
        layer_out[None],
        input_grad[None],
        sum_gain_first,
        sum_shift_first,
        sum_qkv,
        sum_bias_qv,
        sum_out,
        sum_bias_out,
        sum_gain_second,
        sum_shift_second,
        sum_up,
        sum_bias_up,
        sum_down,
        sum_bias_down,
    )


def solution(mesh):
    placed = (
        P("dp", "ctx", None),
        P("dp"),
        P(("dp", "ctx")),
        P(("dp", "ctx")),
        P(("dp", "ctx"), None),
        P(("dp", "ctx")),
        P(("dp", "ctx"), None),
        P(("dp", "ctx")),
        P(("dp", "ctx")),
        P(("dp", "ctx")),
        P(("dp", "ctx"), None),
        P(("dp", "ctx")),
        P(("dp", "ctx"), None),
        P(("dp", "ctx")),
        P("dp", "ctx", None),
    )
    return jax.shard_map(
        per_device,
        mesh=mesh,
        in_specs=placed,
        out_specs=(
            P("dp", "ctx", None),
            P("dp", "ctx", None),
            P(("dp", "ctx")),
            P(("dp", "ctx")),
            P(("dp", "ctx"), None),
            P(("dp", "ctx")),
            P(("dp", "ctx"), None),
            P(("dp", "ctx")),
            P(("dp", "ctx")),
            P(("dp", "ctx")),
            P(("dp", "ctx"), None),
            P(("dp", "ctx")),
            P(("dp", "ctx"), None),
            P(("dp", "ctx")),
        ),
        check_vma=False,
    )
```

profile of v0, /device:TPU:0, one launch (start us, length us, event | category | flops | bytes accessed | tf_op | source)
XLA Modules:
  0.0 1624.3 jit_solution(12898448946622320328)
XLA Ops:
  13.8 42.5 %all-reduce.16 = (bf16[1024]{0:T(1024)(128)(2,1)S(1)}, bf16[1024]{0:T(1024)(128)(2,1)S(1)}, bf16[2048]{0:T(1024)(128)(2,1)S(1)}, bf16[1024]{0:T(1024)(128)(2,1)S...) all-reduce(bf16[1024]{0:T(1024)(128)(2,1)S(1)} %dynamic-update-slic, ...), channel_id=1, replica_groups=mesh['dp'=8,'ctx'=4] {'dp','ctx'}, use_global_device_ids=true, to_apply=%add.1 | all-reduce | flops 8192 | bytes 32768
  59.5 23.9 %all-gather.8.cloned.1.call-done = bf16[1024,3072]{1,0:T(8,128)(2,1)} async-done(((bf16[32,3072]{1,0:T(8,128)(2,1)}), bf16[1024,3072]{1,0:T(8,128)(2,1)}) %all-gather.8.cloned.1.call-update) | async-done | bytes 6291472 | tf_op jit(solution)/shard_map/all_gather | solution.py:72
  92.4 66.2 %all-gather = bf16[32,1,128]{2,1,0:T(2,128)(2,1)S(1)} all-gather(bf16[1,1,128]{2,1,0:T(2,128)(2,1)S(1)} %bitcast.227), channel_id=1, replica_groups=mesh['dp'=8,'ctx'=4] {'dp','ctx'}, dimensions={0}, use_global_device_ids=true | all-gather | bytes 8448 | tf_op jit(solution)/shard_map/all_gather | solution.py:79
  171.8 9.4 all-gather.12.cloned.1.call-done
  192.1 24.0 %while.39 = (s32[]{:T(128)}, f32[16,256]{1,0:T(8,128)S(1)}, f32[16,256]{1,0:T(8,128)S(1)}, s32[2]{0:T(128)S(1)}, s32[]{:T(128)}, /*index=5*/bf16[2,512,16,64]{1,...) while((s32[]{:T(128)}, f32[16,256]{1,0:T(8,128)S(1)}, ...), condition=%wide.region_5.6_spmd.clone, body=%wide.region_2.5_spmd.clone.sunk | while | flops 285497088 | bytes 18963608 | solution.py:125
  216.2 16.0 while.40
  243.3 75.1 %all-gather.16.cloned.1.call-done = bf16[1024,4096]{1,0:T(8,128)(2,1)} async-done(((bf16[32,4096]{1,0:T(8,128)(2,1)}), bf16[1024,4096]{1,0:T(8,128)(2,1)}) %all-gather.16.cloned.1.call-update) | async-done | bytes 8388624 | tf_op jit(solution)/shard_map/all_gather | solution.py:78
  318.4 8.2 convolution_add_fusion
  326.7 70.6 %all-gather.18.cloned.1.call-done = bf16[4096,1024]{1,0:T(8,128)(2,1)} async-done(((bf16[128,1024]{1,0:T(8,128)(2,1)}), bf16[4096,1024]{1,0:T(8,128)(2,1)}) %all-gather.18.cloned.1.call-update) | async-done | bytes 8388624 | tf_op jit(solution)/shard_map/all_gather | solution.py:80
  397.2 8.9 convert_reduce_fusion
  418.8 63.5 %while.41 = (s32[]{:T(128)}, f32[256,16,64]{0,2,1:T(8,128)}, bf16[2,512,1024]{2,1,0:T(8,128)(2,1)}, bf16[2,512,1024]{2,1,0:T(8,128)(2,1)}, bf16[2,512,16,64]{1,3...) while((s32[]{:T(128)}, f32[256,16,64]{0,2,1:T(8,128)}, ...), condition=%wide.region_14.15_spmd.clone, body=%wide.region_13.14_spmd.clone.sunk | while | flops 1369442048 | bytes 102161728 | solution.py:227
  431.7 6.5 fusion.181
  463.5 6.5 fusion.181
  494.3 34.7 %reduce-scatter.9.cloned.1.call-done = bf16[256,1024]{0,1:T(8,128)(2,1)} async-done(((bf16[1024,1024]{0,1:T(8,128)(2,1)}), bf16[256,1024]{0,1:T(8,128)(2,1)}) %reduce-scatter.9.cloned.1.call-update) | async-done | bytes 524304 | tf_op jit(solution)/shard_map/reduce_scatter | solution.py:237
  529.0 45.6 %reduce-scatter.7.cloned.1.call-done = bf16[256,1024]{0,1:T(8,128)(2,1)} async-done(((bf16[1024,1024]{0,1:T(8,128)(2,1)}), bf16[256,1024]{0,1:T(8,128)(2,1)}) %reduce-scatter.7.cloned.1.call-update) | async-done | bytes 524304 | tf_op jit(solution)/shard_map/reduce_scatter | solution.py:231
  574.6 7.7 fusion.93
  583.6 9.8 fusion.109
  594.5 10.7 fusion.95
  606.0 8.3 fusion.82
  621.6 41.2 %all-reduce.15 = (f32[1024]{0:T(1024)S(1)}, f32[1024]{0:T(1024)S(1)}, f32[2048]{0:T(1024)S(1)}, f32[1024]{0:T(1024)S(1)}, f32[1024]{0:T(1024)S(1)}, /*index=5*/f...) all-reduce(f32[1024]{0:T(1024)S(1)} %get-tuple-element.430, ...), channel_id=4, replica_groups=mesh['dp'=8,'ctx'=4] {'dp','ctx'}, use_global_device_ids=true, to_apply=%region_20.21.clone | all-reduce | flops 12288 | bytes 98304
  667.5 58.1 %reduce-scatter.13.cloned.1.call-done = f32[32,1024]{1,0:T(8,128)} async-done(((f32[1024,1024]{1,0:T(8,128)}), f32[32,1024]{1,0:T(8,128)}) %reduce-scatter.13.cloned.1.call-update) | async-done | bytes 131088 | tf_op jit(solution)/shard_map/reduce_scatter | solution.py:281
  725.6 160.3 %reduce-scatter.11.cloned.1.call-done = f32[32,3072]{1,0:T(8,128)} async-done(((f32[1024,3072]{1,0:T(8,128)}), f32[32,3072]{1,0:T(8,128)}) %reduce-scatter.11.cloned.1.call-update) | async-done | bytes 393232 | tf_op jit(solution)/shard_map/reduce_scatter | solution.py:279
  885.9 366.3 %reduce-scatter.15.cloned.1.call-done = f32[32,4096]{1,0:T(8,128)} async-done(((f32[1024,4096]{1,0:T(8,128)}), f32[32,4096]{1,0:T(8,128)}) %reduce-scatter.15.cloned.1.call-update) | async-done | bytes 524304 | tf_op jit(solution)/shard_map/reduce_scatter | solution.py:285
  1252.2 365.0 %reduce-scatter.17.cloned.1.call-done = f32[128,1024]{1,0:T(8,128)} async-done(((f32[4096,1024]{1,0:T(8,128)}), f32[128,1024]{1,0:T(8,128)}) %reduce-scatter.17.cloned.1.call-update) | async-done | bytes 524304 | tf_op jit(solution)/shard_map/reduce_scatter | solution.py:287
  (247 shorter events, 183.1 us)
Async XLA Ops:
  7.2 76.2 %all-gather.8.cloned.1.call-start = ((), (), s32[]{:S(2)}) async-start(), calls=%async_computation.6 | async-start | bytes 6488064 | tf_op jit(solution)/shard_map/all_gather | solution.py:72
  7.9 152.0 %all-gather.10.cloned.1.call-start = ((), (), s32[]{:S(2)}) async-start(), calls=%async_computation.7 | async-start | bytes 2621440 | tf_op jit(solution)/shard_map/all_gather | solution.py:105
  56.4 31.9 %copy-start.24 = (f32[1024]{0:T(1024)}, f32[1024]{0:T(1024)S(1)}, u32[]{:S(2)}) copy-start(f32[1024]{0:T(1024)S(1)} %convert_element_type.122) | copy-start | bytes 12292
  56.4 31.9 %copy-start.22 = (f32[1024]{0:T(1024)}, f32[1024]{0:T(1024)S(1)}, u32[]{:S(2)}) copy-start(f32[1024]{0:T(1024)S(1)} %convert_element_type.121) | copy-start | bytes 12292
  57.6 30.7 %copy-start.26 = (f32[256]{0:T(256)}, f32[256]{0:T(256)S(1)}, u32[]{:S(2)}) copy-start(f32[256]{0:T(256)S(1)} %broadcast_multiply_fusion.1) | copy-start | bytes 3076
  58.9 29.3 %copy-start.28 = (f32[256]{0:T(256)}, f32[256]{0:T(256)S(1)}, u32[]{:S(2)}) copy-start(f32[256]{0:T(256)S(1)} %fusion.101) | copy-start | bytes 3076
  89.6 91.7 %all-gather.12.cloned.1.call-start = ((), (), s32[]{:S(2)}) async-start(), calls=%async_computation.8 | async-start | bytes 2621440 | tf_op jit(solution)/shard_map/all_gather | solution.py:104
  90.5 148.9 %all-gather.14.cloned.1.call-start = ((), (), s32[]{:S(2)}) async-start(), calls=%async_computation.9 | async-start | bytes 2162688 | tf_op jit(solution)/shard_map/all_gather | solution.py:74
  91.1 227.3 %all-gather.16.cloned.1.call-start = ((), (), s32[]{:S(2)}) async-start(), calls=%async_computation.10 | async-start | bytes 8650752 | tf_op jit(solution)/shard_map/all_gather | solution.py:78
  91.7 305.6 %all-gather.18.cloned.1.call-start = ((), (), s32[]{:S(2)}) async-start(), calls=%async_computation.11 | async-start | bytes 8650752 | tf_op jit(solution)/shard_map/all_gather | solution.py:80
  92.2 436.8 %reduce-scatter.9.cloned.1.call-start = ((), (), s32[]{:S(2)}) async-start(), calls=%async_computation.13 | async-start | bytes 2621440 | tf_op jit(solution)/shard_map/reduce_scatter | solution.py:237
  216.2 23.2 %copy-start.2 = (bf16[1,256,1024]{2,1,0:T(8,128)(2,1)S(1)}, bf16[1,256,1024]{2,1,0:T(8,128)(2,1)}, u32[]{:S(2)}) copy-start(bf16[1,256,1024]{2,1,0:T(8,128)(2,1)} %param.21) | copy-start | bytes 1572868
  397.2 10.3 copy-start.4
  397.2 10.3 copy-start.40
  486.4 88.2 %reduce-scatter.7.cloned.1.call-start = ((), (), s32[]{:S(2)}) async-start(), calls=%async_computation.12 | async-start | bytes 2621440 | tf_op jit(solution)/shard_map/reduce_scatter | solution.py:231
  489.0 236.6 %reduce-scatter.13.cloned.1.call-start = ((), (), s32[]{:S(2)}) async-start(), calls=%async_computation.15 | async-start | bytes 4325376 | tf_op jit(solution)/shard_map/reduce_scatter | solution.py:281
  492.8 81.8 %copy-start.23 = (f32[1024]{0:T(1024)S(1)}, f32[1024]{0:T(1024)}, u32[]{:S(2)}) copy-start(f32[1024]{0:T(1024)} %copy-done.22) | copy-start | bytes 12292
  492.8 81.8 %copy-start.25 = (f32[1024]{0:T(1024)S(1)}, f32[1024]{0:T(1024)}, u32[]{:S(2)}) copy-start(f32[1024]{0:T(1024)} %copy-done.24) | copy-start | bytes 12292
  492.8 81.8 %copy-start.27 = (f32[256]{0:T(256)S(1)}, f32[256]{0:T(256)}, u32[]{:S(2)}) copy-start(f32[256]{0:T(256)} %copy-done.26) | copy-start | bytes 3076
  492.8 81.8 %copy-start.29 = (f32[256]{0:T(256)S(1)}, f32[256]{0:T(256)}, u32[]{:S(2)}) copy-start(f32[256]{0:T(256)} %copy-done.28) | copy-start | bytes 3076
  492.9 393.0 %reduce-scatter.11.cloned.1.call-start = ((), (), s32[]{:S(2)}) async-start(), calls=%async_computation.14 | async-start | bytes 12976128 | tf_op jit(solution)/shard_map/reduce_scatter | solution.py:279
  494.3 88.1 %copy-start.12 = (bf16[256,16,64]{0,2,1:T(8,128)(2,1)}, bf16[256,16,64]{0,2,1:T(8,128)(2,1)S(1)}, u32[]{:S(2)}) copy-start(bf16[256,16,64]{0,2,1:T(8,128)(2,1)S(1)} %get-tuple-element.513) | copy-start | bytes 1572868
  582.4 669.8 %reduce-scatter.15.cloned.1.call-start = ((), (), s32[]{:S(2)}) async-start(), calls=%async_computation.16 | async-start | bytes 17301504 | tf_op jit(solution)/shard_map/reduce_scatter | solution.py:285
  593.5 1023.8 %reduce-scatter.17.cloned.1.call-start = ((), (), s32[]{:S(2)}) async-start(), calls=%async_computation.17 | async-start | bytes 17301504 | tf_op jit(solution)/shard_map/reduce_scatter | solution.py:287
  (33 other events, 122.3 us)
Sparse Core Ops, SparseCore 0:
  10.9 72.4 all-gather.7
  89.7 44.6 all-gather.9
  136.5 44.7 all-gather.11
  184.0 55.2 all-gather.13
  242.1 76.2 all-gather.15
  321.2 75.9 all-gather.17
  486.5 42.4 reduce-scatter.8
  531.4 43.1 reduce-scatter.6
  577.5 148.1 reduce-scatter.12
  732.1 153.7 reduce-scatter.10
  888.9 363.2 reduce-scatter.14
  1255.0 362.1 reduce-scatter.16
where the time goes:
time: 1630 us; the launch traced here: 1620 us
  waiting for transfers between devices  1220 us (75%)
  blocking collectives  150 us (9%)
  matrix products  137 us (8%)
  local copies, waits for them, and re-layouts  71.8 us (4%)
  other arithmetic  33.5 us (2%)
    reduce_scatter x1, waiting for transfers between devices, per_device(): lax.psum_scatter(grad_proj_up, ('dp', 'ctx'), scatter_dimension=0, tiled=...  366 us
    reduce_scatter x1, waiting for transfers between devices, per_device(): lax.psum_scatter(grad_proj_down, ('dp', 'ctx'), scatter_dimension=0, tile...  365 us
    reduce_scatter x1, waiting for transfers between devices, per_device(): lax.psum_scatter(grad_proj_qkv, ('dp', 'ctx'), scatter_dimension=0, tiled...  160 us
    unnamed x2, blocking collectives  83.7 us
    all_gather x1, waiting for transfers between devices, per_device(): lax.all_gather(w_up, ('dp', 'ctx'), axis=0, tiled=True)  75.1 us
    all_gather x1, waiting for transfers between devices, per_device(): lax.all_gather(w_down, ('dp', 'ctx'), axis=0, tiled=True)  70.6 us
    all_gather x1, blocking collectives, per_device(): lax.all_gather(b_up, ('dp', 'ctx'), axis=0, tiled=True)  66.2 us
    reduce_scatter x1, waiting for transfers between devices, per_device(): lax.psum_scatter(grad_proj_out, ('dp', 'ctx'), scatter_dimension=0, tiled...  58.1 us
  transfers between devices with their start and end apart: 12, of which 11 were waited for; matrix products, arithmetic and copies ran while one was open for 9% of the time, Pallas kernels for 0%

commit v1 on v0

v1 whole, which is shorter than its diff:
```python
import functools

import jax
import jax.numpy as jnp
from jax import lax
from jax.experimental import pallas as pl
from jax.experimental.pallas import tpu as pltpu
from jax.sharding import PartitionSpec as P

HEADS = 16
HD = 64
SCALE = 0.125
NEGATIVE = -1e30
AXES = ("dp", "ctx")
F32 = jnp.float32
BF16 = jnp.bfloat16


def dot_nt(a, b):
    return lax.dot_general(a, b, (((1,), (1,)), ((), ())), preferred_element_type=F32)


def dot_tn(a, b):
    return lax.dot_general(a, b, (((0,), (0,)), ((), ())), preferred_element_type=F32)


def dot_nn(a, b):
    return lax.dot_general(a, b, (((1,), (0,)), ((), ())), preferred_element_type=F32)


def allowed_keys(limit, rows, first_query, prefix_len):
    key_pos = lax.broadcasted_iota(jnp.int32, (limit, rows), 0)
    query_pos = lax.broadcasted_iota(jnp.int32, (limit, rows), 1) + first_query
    return (key_pos <= query_pos) | (key_pos < prefix_len)


def over_blocks(length, rows, step):
    if length <= 1024:
        for first in range(0, length, rows):
            step(first, max(length // 2, first + rows))
    else:

        def body(i, carry):
            step(pl.multiple_of(i * rows, rows), length)
            return carry

        lax.fori_loop(0, length // rows, body, 0)


def attend_forward(prefix_ref, q_ref, k_ref, v_ref, o_ref, lse_ref, *, rows):
    length, width = q_ref.shape
    group = width // HD
    prefix_len = prefix_ref[0]
    lane_head = lax.broadcasted_iota(jnp.int32, (1, width), 1) // HD

    def step(first, limit):
        block = pl.ds(first, rows)
        queries = q_ref[block, :] * SCALE
        keys = k_ref[:limit, :]
        values = v_ref[:limit, :]
        allowed = allowed_keys(limit, rows, first, prefix_len)
        attended = jnp.zeros((rows, width), F32)
        for h in range(group):
            mine = lane_head == h
            scores = dot_nt(keys, jnp.where(mine, queries, 0).astype(BF16))
            scores = jnp.where(allowed, scores, NEGATIVE)
            top = jnp.max(scores, axis=0, keepdims=True)
            terms = jnp.exp(scores - top)
            total = jnp.sum(terms, axis=0, keepdims=True)
            lse_ref[h, :, block] = top + jnp.log(total)
            weights = (terms * (1.0 / total)).astype(BF16)
            attended = jnp.where(mine, dot_tn(weights, values), attended)
        o_ref[block, :] = attended.astype(BF16)

    over_blocks(length, rows, step)


def attend_backward(
    prefix_ref, q_ref, k_ref, v_ref, o_ref, do_ref, lse_ref, dq_ref, dk_ref, dv_ref, dk_sum, dv_sum, *, rows
):
    length, width = q_ref.shape
    group = width // HD
    prefix_len = prefix_ref[0]
    lane_head = lax.broadcasted_iota(jnp.int32, (1, width), 1) // HD
    dk_sum[...] = jnp.zeros_like(dk_sum)
    dv_sum[...] = jnp.zeros_like(dv_sum)

    def step(first, limit):
        block = pl.ds(first, rows)
        queries = q_ref[block, :] * SCALE
        grads = do_ref[block, :]
        keys = k_ref[:limit, :]
        values = v_ref[:limit, :]
        allowed = allowed_keys(limit, rows, first, prefix_len)
        products = (grads.astype(F32) * o_ref[block, :].astype(F32)).T
        query_grad = jnp.zeros((rows, width), F32)
        for h in range(group):
            mine = lane_head == h
            queries_h = jnp.where(mine, queries, 0).astype(BF16)
            grads_h = jnp.where(mine, grads, 0).astype(BF16)
            delta = jnp.sum(products[h * HD : (h + 1) * HD, :], axis=0, keepdims=True)
            scores = jnp.where(allowed, dot_nt(keys, queries_h), NEGATIVE)
            probs = jnp.exp(scores - lse_ref[h, :, block])
            weight_grad = dot_nt(values, grads_h)
            score_grad = (probs * (weight_grad - delta)).astype(BF16)
            dv_sum[:limit, :] += dot_nn(probs.astype(BF16), grads_h)
            dk_sum[:limit, :] += dot_nn(score_grad, queries_h)
            query_grad = jnp.where(mine, dot_tn(score_grad, keys), query_grad)
        dq_ref[block, :] = (query_grad * SCALE).astype(BF16)

    over_blocks(length, rows, step)
    dk_ref[...] = dk_sum[...].astype(BF16)
    dv_ref[...] = dv_sum[...].astype(BF16)


def attention_shapes(mixed):
    length, width = mixed.shape
    heads = width // (3 * HD)
    group = 2 if heads % 2 == 0 else 1
    return length, heads, group, heads // group, group * HD


def thirds(mixed, count, lanes):
    length, width = mixed.shape
    part = lambda n: pl.BlockSpec((length, lanes), lambda g: (0, n * count + g))
    if lanes % 128 == 0:
        return [mixed] * 3, [part(0), part(1), part(2)]
    return [mixed[:, n * width // 3 : (n + 1) * width // 3] for n in range(3)], [part(0)] * 3


def attention(prefix, mixed):
    length, heads, group, count, lanes = attention_shapes(mixed)
    operands, columns = thirds(mixed, count, lanes)
    return pl.pallas_call(
        functools.partial(attend_forward, rows=min(256, length)),
        grid=(count,),
        in_specs=[pl.BlockSpec(memory_space=pltpu.SMEM)] + columns,
        out_specs=[
            pl.BlockSpec((length, lanes), lambda g: (0, g)),
            pl.BlockSpec((group, 1, length), lambda g: (g, 0, 0)),
        ],
        out_shape=[
            jax.ShapeDtypeStruct((length, heads * HD), BF16),
            jax.ShapeDtypeStruct((heads, 1, length), F32),
        ],
        compiler_params=pltpu.CompilerParams(vmem_limit_bytes=48 * 2**20),
        name="attend_forward",
    )(prefix, *operands)


def attention_grads(prefix, mixed, attended, grad_attended, log_total):
    length, heads, group, count, lanes = attention_shapes(mixed)
    operands, columns = thirds(mixed, count, lanes)
    own = pl.BlockSpec((length, lanes), lambda g: (0, g))
    wide = jax.ShapeDtypeStruct((length, heads * HD), BF16)
    return pl.pallas_call(
        functools.partial(attend_backward, rows=min(256, length)),
        grid=(count,),
        in_specs=[
            pl.BlockSpec(memory_space=pltpu.SMEM),
            *columns,
            own,
            own,
            pl.BlockSpec((group, 1, length), lambda g: (g, 0, 0)),
        ],
        out_specs=[own] * 3,
        out_shape=[wide] * 3,
        scratch_shapes=[pltpu.VMEM((length, lanes), F32)] * 2,
        compiler_params=pltpu.CompilerParams(vmem_limit_bytes=48 * 2**20),
        name="attend_backward",
    )(prefix, *operands, attended, grad_attended, log_total)


def bits_of(size):
    return size.bit_length() - 1


def rank(bit):
    return (0 if bit[0] == "ctx" else 1, bit[1])


def my_bit(bit):
    return (lax.axis_index(bit[0]) >> bit[1]) & 1


def swap_by(x, dp_mask, ctx_mask):
    dp, ctx = lax.axis_size("dp"), lax.axis_size("ctx")
    pairs = [
        (d * ctx + c, (d ^ dp_mask) * ctx + (c ^ ctx_mask)) for d in range(dp) for c in range(ctx)
    ]
    return lax.ppermute(x, AXES, pairs)


def swap(x, bit):
    return swap_by(x, 1 << bit[1], 0) if bit[0] == "dp" else swap_by(x, 0, 1 << bit[1])


def join(own, other, here, axis):
    first = here == 0
    return jnp.stack([jnp.where(first, own, other), jnp.where(first, other, own)], axis)


def gather(x, bits, done=()):
    done = list(done)
    for bit in bits:
        place = sum(rank(d) > rank(bit) for d in done)
        x = join(x, swap(x, bit), my_bit(bit), place)
        done.append(bit)
    return x


def scatter(x, bits, left=()):
    remaining = sorted(list(bits) + list(left), key=rank, reverse=True)
    for n, bit in enumerate(bits):
        place = remaining.index(bit)
        here = my_bit(bit)
        sent = lax.dynamic_index_in_dim(x, 1 - here, place, keepdims=False)
        kept = lax.dynamic_index_in_dim(x, here, place, keepdims=False)
        x = kept.astype(F32) + swap(sent, bit).astype(F32)
        remaining.pop(place)
        if n + 1 < len(bits):
            x = x.astype(sent.dtype)
    return x


def unrelate(pieces):
    me = lax.axis_index("ctx")
    for b in range(bits_of(len(pieces))):
        flip = ((me >> b) & 1) == 1
        pieces = [jnp.where(flip, pieces[j ^ (1 << b)], pieces[j]) for j in range(len(pieces))]
    return pieces


def gather_ctx(x):
    return unrelate([x] + [swap_by(x, 0, s) for s in range(1, lax.axis_size("ctx"))])


def exchange_ctx(x):
    me = lax.axis_index("ctx")
    pick = lambda j: lax.dynamic_index_in_dim(x, j, 0, keepdims=False)
    return unrelate(
        [pick(me)] + [swap_by(pick(me ^ s), 0, s) for s in range(1, lax.axis_size("ctx"))]
    )


def sum_ctx(x):
    me = lax.axis_index("ctx")
    pick = lambda j: lax.dynamic_index_in_dim(x, j, 0, keepdims=False)
    total = pick(me).astype(F32)
    for s in range(1, lax.axis_size("ctx")):
        total = total + swap_by(pick(me ^ s).astype(BF16), 0, s).astype(F32)
    return total


def normalize(values):
    center = jnp.mean(values, axis=-1, keepdims=True)
    offsets = values - center
    spread = jnp.mean(offsets * offsets, axis=-1, keepdims=True)
    scale = lax.rsqrt(spread + 1e-05)
    return offsets * scale, scale


def norm_back(grad, gain, hat, scale):
    e = grad * gain
    return scale * (
        e
        - jnp.mean(e, axis=-1, keepdims=True)
        - hat * jnp.mean(e * hat, axis=-1, keepdims=True)
    )


def gelu_tanh(values):
    return jax.nn.gelu(values, approximate=True)


def per_device(
    layer_input,
    prefix,
    ln1_gain,
    ln1_bias,
    w_qkv,
    b_qv,
    w_out,
    b_out,
    ln2_gain,
    ln2_bias,
    w_up,
    b_up,
    w_down,
    b_down,
    cotangent,
):
    dp, ctx = lax.axis_size("dp"), lax.axis_size("ctx")
    devices = dp * ctx
    planes = dp // 2
    tokens, d = layer_input.shape[1:]
    length = tokens * ctx
    width = HEADS * HD // ctx
    ff = b_up.shape[0] * devices
    chunk = ff // 4
    piece = b_up.shape[0] // 2
    rows = d // devices
    core_bit = ("dp", 0)
    plane_bits = [("dp", b) for b in range(1, bits_of(dp))]
    ctx_bits = [("ctx", b) for b in range(bits_of(ctx))]
    twos = lambda bits: (2,) * len(bits)
    core = my_bit(core_bit)
    z = lax.axis_index("ctx")
    x_own = layer_input[0]
    cot_own = cotangent[0]

    small = [ln1_gain, ln1_bias, b_qv, b_out, ln2_gain, ln2_bias, b_up, b_down]
    sizes = [s.shape[0] for s in small]
    packed = gather(jnp.concatenate(small)[None], ctx_bits + [core_bit] + plane_bits)
    packed = packed.reshape(devices, sum(sizes))
    whole = []
    start = 0
    for size in sizes:
        whole.append(packed[:, start : start + size].reshape(devices * size).astype(F32))
        start += size
    gain_first, shift_first, bias_qv, bias_out, gain_second, shift_second, bias_up, bias_down = whole

    by_head = w_qkv.reshape(rows, 3, ctx, width).transpose(2, 0, 1, 3).reshape(ctx, rows, 3 * width)
    own_cols = jnp.stack(exchange_ctx(by_head), 0)
    proj_qkv = gather(own_cols, plane_bits + [core_bit]).reshape(d, 3 * width)

    inputs_all = jnp.concatenate(gather_ctx(x_own), 0)

    up_cols = w_up.reshape(rows, planes, 2, ctx, 2, piece)
    up_pair = join(
        lax.dynamic_index_in_dim(up_cols, core, 2, keepdims=False),
        swap(lax.dynamic_index_in_dim(up_cols, 1 - core, 2, keepdims=False), core_bit),
        core,
        0,
    )
    orders = (plane_bits, plane_bits[::-1])
    proj_up, proj_down, bias_ups = [], [], []
    bias_up_core = lax.dynamic_index_in_dim(
        bias_up.reshape(planes, 2, ctx, 2, piece), core, 1, keepdims=False
    )
    for c in range(2):
        part = up_pair[:, :, :, :, c].reshape(2, rows, planes * ctx * piece)
        proj_up.append(gather(part, ctx_bits + orders[c], [core_bit]).reshape(d, chunk))
        part = w_down[c * piece : (c + 1) * piece]
        proj_down.append(gather(part, ctx_bits + orders[c]).reshape(chunk, d))
        bias_ups.append(bias_up_core[:, :, c].reshape(chunk))
    proj_out = gather(w_out, ctx_bits + plane_bits[::-1] + [core_bit]).reshape(d, d)

    hat_all, scale_all = normalize(inputs_all.astype(F32))
    hidden_first = (hat_all * gain_first + shift_first).astype(BF16)
    mixed = jnp.dot(hidden_first, proj_qkv, preferred_element_type=F32)
    bias_heads = lax.dynamic_index_in_dim(bias_qv.reshape(2, ctx, width), z, 1, keepdims=False)
    bias_mixed = jnp.concatenate([bias_heads[0], jnp.zeros((width,), F32), bias_heads[1]])
    mixed = (mixed + bias_mixed).astype(BF16)
    attended_heads, log_total = attention(prefix, mixed)
    attended = jnp.concatenate(exchange_ctx(attended_heads.reshape(ctx, tokens, width)), 1)

    inputs = x_own.astype(F32)
    resid = inputs + jnp.dot(attended, proj_out, preferred_element_type=F32) + bias_out
    hat_second, scale_second = normalize(resid)
    hidden_second = (hat_second * gain_second + shift_second).astype(BF16)

    pair = lambda t: jnp.concatenate([t, swap(t, core_bit)], 0)
    hidden_pair = pair(hidden_second)
    cot_pair = pair(cot_own)
    split_sum = lambda t: t[:tokens] + swap(t[tokens:].astype(BF16), core_bit).astype(F32)
    out_part = 0.0
    grad_hidden_part = 0.0
    grads_down, grads_up, grads_bias_up = [], [], []
    for c in range(2):
        pre_act = (
            jnp.dot(hidden_pair, proj_up[c], preferred_element_type=F32) + bias_ups[c]
        )
        gelu_value, gelu_pull = jax.vjp(gelu_tanh, pre_act)
        activ = gelu_value.astype(BF16)
        out_part += jnp.dot(activ, proj_down[c], preferred_element_type=F32)
        grad_activ = dot_nt(cot_pair, proj_down[c])
        grad_pre = gelu_pull(grad_activ)[0].astype(BF16)
        grads_bias_up.append(jnp.sum(grad_pre.astype(F32), axis=0))
        grad_hidden_part += dot_nt(grad_pre, proj_up[c])
        grad = dot_tn(activ, cot_pair).astype(BF16)
        grad = grad.reshape(twos(plane_bits) + twos(ctx_bits) + (piece, d))
        grads_down.append(scatter(grad, orders[c] + ctx_bits[::-1]))
        grad = dot_tn(hidden_pair, grad_pre).astype(BF16)
        grad = grad.reshape(twos(plane_bits) + (2,) + twos(ctx_bits) + (rows, chunk))
        grads_up.append(scatter(grad, orders[c] + ctx_bits[::-1], [core_bit]))
    layer_out = (resid + split_sum(out_part) + bias_down).astype(BF16)
    sum_down = jnp.concatenate(grads_down, 0)
    up_sum = jnp.stack([g.reshape(2, rows, planes, ctx, piece) for g in grads_up], 4)
    sum_up = join(
        lax.dynamic_index_in_dim(up_sum, core, 0, keepdims=False),
        swap(lax.dynamic_index_in_dim(up_sum, 1 - core, 0, keepdims=False).astype(BF16), core_bit).astype(F32),
        core,
        2,
    ).reshape(rows, ff)

    grad_hidden_second = split_sum(grad_hidden_part)
    upstream = cot_own.astype(F32)
    grad_gain_second = jnp.sum(grad_hidden_second * hat_second, axis=0)
    grad_shift_second = jnp.sum(grad_hidden_second, axis=0)
    grad_resid = upstream + norm_back(grad_hidden_second, gain_second, hat_second, scale_second)
    grad_branch = grad_resid.astype(BF16)
    grad_bias_out = jnp.sum(grad_branch.astype(F32), axis=0)
    grad_attended = dot_nt(grad_branch, proj_out).astype(BF16)
    grad_heads = jnp.concatenate(
        exchange_ctx(grad_attended.reshape(tokens, ctx, width).transpose(1, 0, 2)), 0
    )
    grad_out = dot_tn(attended, grad_branch).astype(BF16)
    grad_out = grad_out.reshape(twos(plane_bits) + (2,) + twos(ctx_bits) + (rows, d))
    sum_out = scatter(grad_out, [core_bit] + plane_bits + ctx_bits[::-1])

    grad_q, grad_k, grad_v = attention_grads(prefix, mixed, attended_heads, grad_heads, log_total)
    grad_mixed = jnp.concatenate([grad_q, grad_k, grad_v], 1)
    grad_hidden_all = dot_nt(grad_mixed, proj_qkv)
    grad_qkv = dot_tn(hidden_first, grad_mixed).astype(BF16)
    grad_qkv = grad_qkv.reshape((2,) * bits_of(dp) + (ctx * rows, 3 * width))
    own_rows = scatter(grad_qkv, [core_bit] + plane_bits).astype(BF16)
    columns = exchange_ctx(own_rows.reshape(ctx, rows, 3 * width))
    sum_qkv = (
        jnp.stack([c.reshape(rows, 3, width) for c in columns], 2)
        .reshape(rows, 3 * d)
        .astype(F32)
    )

    grad_gain_first = jnp.sum(grad_hidden_all * hat_all, axis=0)
    grad_shift_first = jnp.sum(grad_hidden_all, axis=0)
    grad_hidden_first = sum_ctx(grad_hidden_all.reshape(ctx, tokens, d))
    hat_first, scale_first = normalize(inputs)
    input_grad = grad_resid + norm_back(grad_hidden_first, gain_first, hat_first, scale_first)

    sums_heads = jnp.sum(grad_mixed.astype(F32), axis=0).reshape(3, 1, width)
    at_heads = lambda t: lax.dynamic_update_slice(jnp.zeros((1, ctx, width), F32), t[None], (0, z, 0))
    grad_bias_qv = jnp.concatenate([at_heads(sums_heads[0]), at_heads(sums_heads[2])], 0)
    up_own = jnp.stack([g.reshape(planes, 1, ctx, piece) for g in grads_bias_up], 3)
    grad_bias_up = lax.dynamic_update_slice(
        jnp.zeros((planes, 2, ctx, 2, piece), F32), up_own, (0, core, 0, 0, 0)
    )
    grad_bias_down = jnp.sum(upstream, axis=0)
    grads = [
        grad_gain_first,
        grad_shift_first,
        grad_bias_qv,
        grad_bias_out,
        grad_gain_second,
        grad_shift_second,
        grad_bias_up,
        grad_bias_down,
    ]
    packed = jnp.concatenate([g.reshape(devices, size) for g, size in zip(grads, sizes)], 1)
    packed = packed.reshape((2,) * bits_of(devices) + (1, sum(sizes)))
    packed = scatter(packed, plane_bits + [core_bit] + ctx_bits)[0]
    sums = []
    start = 0
    for size in sizes:
        sums.append(packed[start : start + size])
        start += size
    (
        sum_gain_first,
        sum_shift_first,
        sum_bias_qv,
        sum_bias_out,
        sum_gain_second,
        sum_shift_second,
        sum_bias_up,
        sum_bias_down,
    ) = sums
    return (
        layer_out[None],
        input_grad[None],
        sum_gain_first,
        sum_shift_first,
        sum_qkv,
        sum_bias_qv,
        sum_out,
        sum_bias_out,
        sum_gain_second,
        sum_shift_second,
        sum_up,
        sum_bias_up,
        sum_down,
        sum_bias_down,
    )


def solution(mesh):
    vector = P(AXES)
    matrix = P(AXES, None)
    tokens = P("dp", "ctx", None)
    return jax.shard_map(
        per_device,
        mesh=mesh,
        in_specs=(
            tokens,
            P("dp"),
            vector,
            vector,
            matrix,
            vector,
            matrix,
            vector,
            vector,
            vector,
            matrix,
            vector,
            matrix,
            vector,
            tokens,
        ),
        out_specs=(
            tokens,
            tokens,
            vector,
            vector,
            matrix,
            vector,
            matrix,
            vector,
            vector,
            vector,
            matrix,
            vector,
            matrix,
            vector,
        ),
        check_vma=False,
    )
```

time: 1630 us -> 511 us (0.31)
  waiting for transfers between devices: 1220 us -> 244 us
  blocking collectives: 150 us -> 0 us
  matrix products: 137 us -> 39.3 us
  starting transfers between devices: 0.65 us -> 90.1 us
  Pallas kernels: 0 us -> 16.3 us
    reduce_scatter x6 -> x0, waiting for transfers between devices: 1030 us -> none  [the longest x1 366 us: per_device(): lax.psum_scatter(grad_proj_up, ('dp', 'ctx'), scatter_dimension=0, tiled=...]
    ppermute x0 -> x82, waiting for transfers between devices: none -> 244 us  [swap_by(): return lax.ppermute(x, AXES, pairs)]
    all_gather x6 -> x0, waiting for transfers between devices: 184 us -> none  [the longest x1 75.1 us: per_device(): lax.all_gather(w_up, ('dp', 'ctx'), axis=0, tiled=True)]
    dot_general x26 -> x18, matrix products: 137 us -> 39.3 us  [the longest x6 15.8 us: dot_nt(): lax.dot_general(a, b, (((1,), (1,)), ((), ())), preferred_element_type=F32)]
    ppermute x0 -> x82, starting transfers between devices: none -> 90.1 us  [swap_by(): return lax.ppermute(x, AXES, pairs)]
    unnamed x2 -> x0, blocking collectives: 83.7 us -> none
    all_gather x1 -> x0, blocking collectives: 66.2 us -> none  [per_device(): lax.all_gather(b_up, ('dp', 'ctx'), axis=0, tiled=True)]
    unnamed x98 -> x166, local copies, waits for them, and re-layouts: 29 us -> 8.58 us
  transfers between devices with their start and end apart: 12 -> 82, of which waited for: 11 -> 38; matrix products, arithmetic and copies ran while one was open for 9% -> 26% of each run, Pallas kernels for 0% -> 3%
where the time goes in v1:
time: 511 us; the launch traced here: 505 us
  waiting for transfers between devices  244 us (48%)
  starting transfers between devices  90.1 us (18%)
  local copies, waits for them, and re-layouts  63.4 us (12%)
  other arithmetic  47.4 us (9%)
  matrix products  39.3 us (8%)
  Pallas kernels  16.3 us (3%)
    ppermute x82, waiting for transfers between devices, swap_by(): return lax.ppermute(x, AXES, pairs)  244 us
    ppermute x82, starting transfers between devices, swap_by(): return lax.ppermute(x, AXES, pairs)  90.1 us
    dot_general x6, matrix products, dot_nt(): lax.dot_general(a, b, (((1,), (1,)), ((), ())), preferred_element_type=F32)  15.8 us
    dot_general x6, matrix products, dot_tn(): lax.dot_general(a, b, (((0,), (0,)), ((), ())), preferred_element_type=F32)  12.6 us
    another operation x62, other arithmetic, join(): jnp.stack([jnp.where(first, own, other), jnp.where(first, other, own)], a...  12.1 us
    concatenate x9, local copies, waits for them, and re-layouts, per_device(): jnp.concatenate([g.reshape(devices, size) for g, size in zip(grads, sizes...  11.9 us
  transfers between devices with their start and end apart: 82, of which 38 were waited for; matrix products, arithmetic and copies ran while one was open for 26% of the time, Pallas kernels for 3%

profile of v1, /device:TPU:0, one launch (start us, length us, event | category | flops | bytes accessed | tf_op | source)
XLA Modules:
  0.0 504.6 jit_solution(16778732929362958684)
XLA Ops:
  0.7 5.1 %collective-permute-start = (bf16[256,1024]{1,0:T(8,128)(2,1)}, bf16[256,1024]{1,0:T(8,128)(2,1)S(1)}, u32[]{:S(2)}, u32[]{:S(2)}) collective-permute-start(bf16[256,1024]{1,0:T(8,128)(2,1)} %bitcast.496), channel_id=1, source_target_pairs={{0,3},{1,2},{2,1},{3,0},{4,7},{5,6},{6,5},{7,4},{8,11},{9,10},{10,... | collective-permute-start | bytes 1572872 | tf_op jit(solution)/shard_map/ppermute | solution.py:191
  5.8 5.4 %concatenate.51 = bf16[384]{0:T(512)(128)(2,1)S(1)} concatenate(bf16[32]{0:T(256)(128)(2,1)} %param.17, bf16[32]{0:T(256)(128)(2,1)} %param.18, bf16[64]{0:T(256)(128)(2,1)} %param.20, bf16[32]{0:T(256)(128)(2,1)} %param.22, bf16[32]{0:T(256)(128)(2,1)} %param.23, bf16[32]{0:T(256)(128)(2,1)} %param.24, bf16[128]{0:T(256)(128)(2,1)} %param.26, bf16[32]{0:T(256)(128)(2,1)} %param.28), dimensions={0} | concatenate | bytes 1536 | tf_op jit(solution)/shard_map/concatenate | solution.py:314
  18.4 11.3 %collective-permute-done.3 = bf16[1,384]{1,0:T(2,128)(2,1)S(1)} collective-permute-done((bf16[1,384]{1,0:T(2,128)(2,1)S(1)}, bf16[1,384]{1,0:T(2,128)(2,1)S(1)}, u32[]{:S(2)}, u32[]{:S(2)}) %collective-permute-start.3) | collective-permute-done | bytes 800 | tf_op jit(solution)/shard_map/ppermute | solution.py:191
  30.7 24.4 %collective-permute-done.4 = bf16[2,1,384]{2,0,1:T(2,128)(2,1)S(1)} collective-permute-done((bf16[2,1,384]{2,0,1:T(2,128)(2,1)S(1)}, bf16[2,1,384]{2,0,1:T(2,128)(2,1)S(1)}, u32[]{:S(2)}, u32[]{:S(2)}) %collective-permute-start.4) | collective-permute-done | bytes 1568 | tf_op jit(solution)/shard_map/ppermute | solution.py:191
  72.2 9.8 %collective-permute-done.17 = bf16[32,1024]{1,0:T(8,128)(2,1)S(1)} collective-permute-done((bf16[32,1024]{1,0:T(8,128)(2,1)S(1)}, bf16[32,1024]{1,0:T(8,128)(2,1)S(1)}, u32[]{:S(2)}, u32[]{:S(2)}) %collective-permute-start.17) | collective-permute-done | bytes 65568 | tf_op jit(solution)/shard_map/ppermute | solution.py:191
  110.2 16.1 %collective-permute-done.29 = bf16[2,64,1024]{2,1,0:T(8,128)(2,1)S(1)} collective-permute-done((bf16[2,64,1024]{2,1,0:T(8,128)(2,1)S(1)}, bf16[2,64,1024]{2,1,0:T(8,128)(2,1)S(1)}, u32[]{:S(2)}, u32[]{:S(2)}) %collective-permute-start.29) | collective-permute-done | bytes 262176 | tf_op jit(solution)/shard_map/ppermute | solution.py:191
  134.4 10.0 %collective-permute-done.33 = bf16[2,2,32,1024]{3,2,1,0:T(8,128)(2,1)S(1)} collective-permute-done((bf16[2,2,32,1024]{3,2,1,0:T(8,128)(2,1)S(1)}, bf16[2,2,32,1024]{3,2,1,0:T(8,128)(2,1)S(1)}, u32[]{:S(2)}, u32[]{:S(2)}) %collective-permute-start.33) | collective-permute-done | bytes 262176 | tf_op jit(solution)/shard_map/ppermute | solution.py:191
  153.0 5.0 collective-permute-done.20
  159.6 9.1 %collective-permute-done.38 = bf16[2,2,64,1024]{3,2,1,0:T(8,128)(2,1)S(1)} collective-permute-done((bf16[2,2,64,1024]{3,2,1,0:T(8,128)(2,1)S(1)}, bf16[2,2,64,1024]{3,2,1,0:T(8,128)(2,1)S(1)}, u32[]{:S(2)}, u32[]{:S(2)}) %collective-permute-start.38) | collective-permute-done | bytes 524320 | tf_op jit(solution)/shard_map/ppermute | solution.py:191
  170.4 4.5 add_convert_fusion.q_ref.k_ref.v_ref
  174.9 7.3 %attend_forward.1 = (bf16[1024,256]{1,0:T(8,128)(2,1)S(1)}, f32[4,1,1024]{2,1,0:T(1,128)S(1)}) custom-call(s32[1]{0:T(128)S(6)} %copy.183.prefix_ref, bf16[1024,768]{1,0:T(8,128)(2,1)S(1)} %add_convert_fusion.q_ref.k_ref.v_ref, bf16[1024,768]{1,0:T(8,128)(2,1)S(1)} %add_convert_fusion.q_ref.k_ref.v_ref, bf16[1024,768]{1,0:T(8,128)(2,1)S(1)} %add_convert_fusion.q_ref.k_ref.v_ref), custom_call_target="tpu_custom_call" | custom-call | tf_op jit(solution)/shard_map/attend_forward/pallas_call | solution.py:134
  182.3 4.6 collective-permute-start.14
  200.6 18.6 %collective-permute-done.35 = bf16[2,2,2,2,32,1024]{5,4,3,1,2,0:T(8,128)(2,1)S(1)} collective-permute-done((bf16[2,2,2,2,32,1024]{5,4,3,1,2,0:T(8,128)(2,1)}, bf16[2,2,2,2,32,1024]{5,4,3,1,2,0:T(8,128)(2,1)S(1)}, u32[]{:S(2)}, u32[]{:S(2)}) %collective-permute-start.35) | collective-permute-done | bytes 1048608 | tf_op jit(solution)/shard_map/ppermute | solution.py:191
  219.5 18.6 %collective-permute-done.39 = bf16[2,2,2,64,1024]{4,3,2,1,0:T(8,128)(2,1)S(1)} collective-permute-done((bf16[2,2,2,64,1024]{4,3,2,1,0:T(8,128)(2,1)}, bf16[2,2,2,64,1024]{4,3,2,1,0:T(8,128)(2,1)S(1)}, u32[]{:S(2)}, u32[]{:S(2)}) %collective-permute-start.39) | collective-permute-done | bytes 1048608 | tf_op jit(solution)/shard_map/ppermute | solution.py:191
  304.3 9.0 %attend_backward.1 = (bf16[1024,256]{1,0:T(8,128)(2,1)S(1)}, bf16[1024,256]{1,0:T(8,128)(2,1)S(1)}, bf16[1024,256]{1,0:T(8,128)(2,1)S(1)}) custom-call(s32[1]{0:T(128)S(6)} %copy.183.prefix_ref, bf16[1024,768]{1,0:T(8,128)(2,1)S(1)} %add_convert_fusion.q_ref.k_ref.v_ref, bf16[1024,768]{1,0:T(8,128)(2,1)S(1)} %add_convert_fusion.q_ref.k_ref.v_ref, ...), custom_call_target="tpu_custom_call" | custom-call | tf_op jit(solution)/shard_map/attend_backward/pallas_call | solution.py:156
  314.8 6.5 %fusion.103 = (f32[1024]{0:T(1024)}, f32[1024]{0:T(1024)}, f32[1024,1024]{1,0:T(8,128)}) fusion(f32[1024]{0:T(1024)S(1)} %copy-done.67, f32[1024]{0:T(1024)S(1)} %copy-done.55, bf16[256,1024]{1,0:T(8,128)(2,1)S(1)} %copy-done.13, bf16[256,1024]{1,0:T(8,128)(2,1)S(1)} %copy-done.11, bf16[256,1024]{1,0:T(8,128)(2,1)S(1)} %copy-done.9, ...), kind=kOutput, calls=%fused_computation.407 | convolution fusion | flops 1624242176 | bytes 9453568 | tf_op jit(solution)/shard_map/dot_general | solution.py:20
  367.0 5.0 collective-permute-done.48
  373.5 30.5 %collective-permute-done.47 = bf16[256,1024]{1,0:T(8,128)(2,1)S(1)} collective-permute-done((bf16[256,1024]{1,0:T(8,128)(2,1)S(1)}, bf16[256,1024]{1,0:T(8,128)(2,1)S(1)}, u32[]{:S(2)}, u32[]{:S(2)}) %collective-permute-start.47) | collective-permute-done | bytes 524320 | tf_op jit(solution)/shard_map/ppermute | solution.py:191
  411.2 7.6 %collective-permute-done.70 = bf16[2,2,2,32,1024]{4,3,2,1,0:T(8,128)(2,1)S(1)} collective-permute-done((bf16[2,2,2,32,1024]{4,3,2,1,0:T(8,128)(2,1)S(1)}, bf16[2,2,2,32,1024]{4,3,2,1,0:T(8,128)(2,1)S(1)}, u32[]{:S(2)}, u32[]{:S(2)}) %collective-permute-start.70) | collective-permute-done | bytes 524320 | tf_op jit(solution)/shard_map/ppermute | solution.py:191
  419.0 11.0 %collective-permute-done.79 = bf16[2,2,64,1024]{3,2,1,0:T(8,128)(2,1)S(1)} collective-permute-done((bf16[2,2,64,1024]{3,2,1,0:T(8,128)(2,1)S(1)}, bf16[2,2,64,1024]{3,2,1,0:T(8,128)(2,1)S(1)}, u32[]{:S(2)}, u32[]{:S(2)}) %collective-permute-start.79) | collective-permute-done | bytes 524320 | tf_op jit(solution)/shard_map/ppermute | solution.py:191
  436.0 17.4 %collective-permute-done.71 = bf16[2,2,32,1024]{3,2,1,0:T(8,128)(2,1)S(1)} collective-permute-done((bf16[2,2,32,1024]{3,2,1,0:T(8,128)(2,1)S(1)}, bf16[2,2,32,1024]{3,2,1,0:T(8,128)(2,1)S(1)}, u32[]{:S(2)}, u32[]{:S(2)}) %collective-permute-start.71) | collective-permute-done | bytes 262176 | tf_op jit(solution)/shard_map/ppermute | solution.py:191
  454.2 4.9 collective-permute-done.80
  459.8 4.8 collective-permute-done.76
  493.4 5.9 %collective-permute-done.63 = bf16[2,32,1024]{2,1,0:T(8,128)(2,1)S(1)} collective-permute-done((bf16[2,32,1024]{2,1,0:T(8,128)(2,1)S(1)}, bf16[2,32,1024]{2,1,0:T(8,128)(2,1)S(1)}, u32[]{:S(2)}, u32[]{:S(2)}) %collective-permute-start.63) | collective-permute-done | bytes 131104 | tf_op jit(solution)/shard_map/ppermute | solution.py:191
  (555 shorter events, 248.5 us)
Async XLA Ops:
  0.7 128.1 %collective-permute-start = (bf16[256,1024]{1,0:T(8,128)(2,1)}, bf16[256,1024]{1,0:T(8,128)(2,1)S(1)}, u32[]{:S(2)}, u32[]{:S(2)}) collective-permute-start(bf16[256,1024]{1,0:T(8,128)(2,1)} %bitcast.496), channel_id=1, source_target_pairs={{0,3},{1,2},{2,1},{3,0},{4,7},{5,6},{6,5},{7,4},{8,11},{9,10},{10,... | collective-permute-start | bytes 1572872 | tf_op jit(solution)/shard_map/ppermute | solution.py:191
  5.8 126.0 %collective-permute-start.1 = (bf16[256,1024]{1,0:T(8,128)(2,1)}, bf16[256,1024]{1,0:T(8,128)(2,1)S(1)}, u32[]{:S(2)}, u32[]{:S(2)}) collective-permute-start(bf16[256,1024]{1,0:T(8,128)(2,1)} %bitcast.497), channel_id=1, source_target_pairs={{0,2},{1,3},{2,0},{3,1},{4,6},{5,7},{6,4},{7,5},{8,10},{9,11},{10,... | collective-permute-start | bytes 1572872 | tf_op jit(solution)/shard_map/ppermute | solution.py:191
  13.4 55.3 %collective-permute-start.8 = (bf16[32,768]{1,0:T(8,128)(2,1)S(1)}, bf16[32,768]{1,0:T(8,128)(2,1)S(1)}, u32[]{:S(2)}, u32[]{:S(2)}) collective-permute-start(bf16[32,768]{1,0:T(8,128)(2,1)S(1)} %get-tuple-element.135), channel_id=1, source_target_pairs={{0,3},{1,2},{2,1},{3,0},{4,7},{5,6},{6,5},{7,4},{8,11},{9,10},{10,... | collective-permute-start | bytes 147464 | tf_op jit(solution)/shard_map/ppermute | solution.py:191
  17.2 53.5 %collective-permute-start.9 = (bf16[32,768]{1,0:T(8,128)(2,1)S(1)}, bf16[32,768]{1,0:T(8,128)(2,1)S(1)}, u32[]{:S(2)}, u32[]{:S(2)}) collective-permute-start(bf16[32,768]{1,0:T(8,128)(2,1)S(1)} %get-tuple-element.134), channel_id=1, source_target_pairs={{0,2},{1,3},{2,0},{3,1},{4,6},{5,7},{6,4},{7,5},{8,10},{9,11},{10,... | collective-permute-start | bytes 147464 | tf_op jit(solution)/shard_map/ppermute | solution.py:191
  68.6 63.2 %collective-permute-start.2 = (bf16[256,1024]{1,0:T(8,128)(2,1)S(1)}, bf16[256,1024]{1,0:T(8,128)(2,1)}, u32[]{:S(2)}, u32[]{:S(2)}) collective-permute-start(bf16[256,1024]{1,0:T(8,128)(2,1)S(1)} %bitcast.498), channel_id=1, source_target_pairs={{0,1},{1,0},{2,3},{3,2},{4,5},{5,4},{6,7},{7,6},{8,9},{9,8},{10,11... | collective-permute-start | bytes 1572872 | tf_op jit(solution)/shard_map/ppermute | solution.py:191
  157.9 37.0 %collective-permute-start.31 = (bf16[2,2,2,64,1024]{4,3,2,1,0:T(8,128)(2,1)}, bf16[2,2,2,64,1024]{4,3,2,1,0:T(8,128)(2,1)S(1)}, u32[]{:S(2)}, u32[]{:S(2)}) collective-permute-start(bf16[2,2,2,64,1024]{4,3,2,1,0:T(8,128)(2,1)} %pad_maximum_fusion.10), channel_id=1, source_target_pairs={{0,16},{1,17},{2,18},{3,19},{4,20},{5,21},{6,22},{7,23},{8,24},{9,... | collective-permute-start | bytes 3145736 | tf_op jit(solution)/shard_map/ppermute | solution.py:191
  158.4 39.5 %collective-permute-start.21 = (bf16[2,2,2,2,32,1024]{5,4,3,2,1,0:T(8,128)(2,1)S(1)}, bf16[2,2,2,2,32,1024]{5,4,3,2,1,0:T(8,128)(2,1)S(1)}, u32[]{:S(2)}, u32[]{:S(2)}) collective-permute-start(bf16[2,2,2,2,32,1024]{5,4,3,2,1,0:T(8,128)(2,1)S(1)} %pad_maximum_fusion.7), channel_id=1, source_target_pairs={{0,4},{1,5},{2,6},{3,7},{4,0},{5,1},{6,2},{7,3},{8,12},{9,13},{10,... | collective-permute-start | bytes 3145736 | tf_op jit(solution)/shard_map/ppermute | solution.py:191
  189.9 52.1 %collective-permute-start.41 = (bf16[256,1024]{1,0:T(8,128)(2,1)S(1)}, bf16[256,1024]{1,0:T(8,128)(2,1)S(1)}, u32[]{:S(2)}, u32[]{:S(2)}) collective-permute-start(bf16[256,1024]{1,0:T(8,128)(2,1)S(1)} %bitcast.528), channel_id=1, source_target_pairs={{0,4},{1,5},{2,6},{3,7},{4,0},{5,1},{6,2},{7,3},{8,12},{9,13},{10,... | collective-permute-start | bytes 1572872 | tf_op jit(solution)/shard_map/ppermute | solution.py:191
  193.3 44.9 %collective-permute-start.39 = (bf16[2,2,2,64,1024]{4,3,2,1,0:T(8,128)(2,1)}, bf16[2,2,2,64,1024]{4,3,2,1,0:T(8,128)(2,1)S(1)}, u32[]{:S(2)}, u32[]{:S(2)}) collective-permute-start(bf16[2,2,2,64,1024]{4,3,2,1,0:T(8,128)(2,1)} %pad_maximum_fusion.12), channel_id=1, source_target_pairs={{0,8},{1,9},{2,10},{3,11},{4,12},{5,13},{6,14},{7,15},{8,0},{9,1},... | collective-permute-start | bytes 3145736 | tf_op jit(solution)/shard_map/ppermute | solution.py:191
  195.0 43.8 %collective-permute-start.27 = (bf16[2,2,2,2,32,1024]{5,4,3,2,1,0:T(8,128)(2,1)S(1)}, bf16[2,2,2,2,32,1024]{5,4,3,2,1,0:T(8,128)(2,1)S(1)}, u32[]{:S(2)}, u32[]{:S(2)}) collective-permute-start(bf16[2,2,2,2,32,1024]{5,4,3,2,1,0:T(8,128)(2,1)S(1)} %pad_maximum_fusion.9), channel_id=1, source_target_pairs={{0,16},{1,17},{2,18},{3,19},{4,20},{5,21},{6,22},{7,23},{8,24},{9,... | collective-permute-start | bytes 3145736 | tf_op jit(solution)/shard_map/ppermute | solution.py:191
  200.5 38.6 %collective-permute-start.22 = (bf16[256,1024]{1,0:T(8,128)(2,1)S(1)}, bf16[256,1024]{1,0:T(8,128)(2,1)S(1)}, u32[]{:S(2)}, u32[]{:S(2)}) collective-permute-start(bf16[256,1024]{1,0:T(8,128)(2,1)S(1)} %add_convert_fusion.1), channel_id=1, source_target_pairs={{0,4},{1,5},{2,6},{3,7},{4,0},{5,1},{6,2},{7,3},{8,12},{9,13},{10,... | collective-permute-start | bytes 1572872 | tf_op jit(solution)/shard_map/ppermute | solution.py:191
  261.2 94.1 %collective-permute-start.65 = (bf16[2,2,2,2,32,1024]{5,4,3,2,1,0:T(8,128)(2,1)}, bf16[2,2,2,2,32,1024]{5,4,3,2,1,0:T(8,128)(2,1)}, u32[]{:S(2)}, u32[]{:S(2)}) collective-permute-start(bf16[2,2,2,2,32,1024]{5,4,3,2,1,0:T(8,128)(2,1)} %dynamic-slice_bitcast_fusion.3), channel_id=1, source_target_pairs={{0,8},{1,9},{2,10},{3,11},{4,12},{5,13},{6,14},{7,15},{8,0},{9,1},... | collective-permute-start | bytes 3145736 | tf_op jit(solution)/shard_map/ppermute | solution.py:191
  265.3 95.2 %collective-permute-start.69 = (bf16[2,2,2,2,32,1024]{5,4,3,2,1,0:T(8,128)(2,1)}, bf16[2,2,2,2,32,1024]{5,4,3,2,1,0:T(8,128)(2,1)}, u32[]{:S(2)}, u32[]{:S(2)}) collective-permute-start(bf16[2,2,2,2,32,1024]{5,4,3,2,1,0:T(8,128)(2,1)} %dynamic-slice_bitcast_fusion.2), channel_id=1, source_target_pairs={{0,16},{1,17},{2,18},{3,19},{4,20},{5,21},{6,22},{7,23},{8,24},{9,... | collective-permute-start | bytes 3145736 | tf_op jit(solution)/shard_map/ppermute | solution.py:191
  300.4 62.0 %collective-permute-start.78 = (bf16[2,2,2,64,1024]{4,3,2,1,0:T(8,128)(2,1)}, bf16[2,2,2,64,1024]{4,3,2,1,0:T(8,128)(2,1)}, u32[]{:S(2)}, u32[]{:S(2)}) collective-permute-start(bf16[2,2,2,64,1024]{4,3,2,1,0:T(8,128)(2,1)} %dynamic-slice_bitcast_fusion), channel_id=1, source_target_pairs={{0,16},{1,17},{2,18},{3,19},{4,20},{5,21},{6,22},{7,23},{8,24},{9,... | collective-permute-start | bytes 3145736 | tf_op jit(solution)/shard_map/ppermute | solution.py:191
  301.4 63.8 %collective-permute-start.74 = (bf16[2,2,2,64,1024]{4,3,2,1,0:T(8,128)(2,1)}, bf16[2,2,2,64,1024]{4,3,2,1,0:T(8,128)(2,1)}, u32[]{:S(2)}, u32[]{:S(2)}) collective-permute-start(bf16[2,2,2,64,1024]{4,3,2,1,0:T(8,128)(2,1)} %dynamic-slice_bitcast_fusion.1), channel_id=1, source_target_pairs={{0,8},{1,9},{2,10},{3,11},{4,12},{5,13},{6,14},{7,15},{8,0},{9,1},... | collective-permute-start | bytes 3145736 | tf_op jit(solution)/shard_map/ppermute | solution.py:191
  353.5 80.0 %collective-permute-start.60 = (bf16[2,2,2,2,32,1024]{5,4,3,2,0,1:T(8,128)(2,1)S(1)}, bf16[2,2,2,2,32,1024]{5,4,3,2,0,1:T(8,128)(2,1)S(1)}, u32[]{:S(2)}, u32[]{:S(2)}) collective-permute-start(bf16[2,2,2,2,32,1024]{5,4,3,2,0,1:T(8,128)(2,1)S(1)} %bitcast.525), channel_id=1, source_target_pairs={{0,4},{1,5},{2,6},{3,7},{4,0},{5,1},{6,2},{7,3},{8,12},{9,13},{10,... | collective-permute-start | bytes 3145736 | tf_op jit(solution)/shard_map/ppermute | solution.py:191
  360.5 43.4 %collective-permute-start.47 = (bf16[256,1024]{1,0:T(8,128)(2,1)S(1)}, bf16[256,1024]{1,0:T(8,128)(2,1)S(1)}, u32[]{:S(2)}, u32[]{:S(2)}) collective-permute-start(bf16[256,1024]{1,0:T(8,128)(2,1)S(1)} %get-tuple-element.43), channel_id=1, source_target_pairs={{0,2},{1,3},{2,0},{3,1},{4,6},{5,7},{6,4},{7,5},{8,10},{9,11},{10,... | collective-permute-start | bytes 1572872 | tf_op jit(solution)/shard_map/ppermute | solution.py:191
  362.4 42.5 %collective-permute-start.46 = (bf16[256,1024]{1,0:T(8,128)(2,1)S(1)}, bf16[256,1024]{1,0:T(8,128)(2,1)S(1)}, u32[]{:S(2)}, u32[]{:S(2)}) collective-permute-start(bf16[256,1024]{1,0:T(8,128)(2,1)S(1)} %get-tuple-element.41), channel_id=1, source_target_pairs={{0,1},{1,0},{2,3},{3,2},{4,5},{5,4},{6,7},{7,6},{8,9},{9,8},{10,11... | collective-permute-start | bytes 1572872 | tf_op jit(solution)/shard_map/ppermute | solution.py:191
  365.2 42.7 %collective-permute-start.54 = (bf16[2,2,128,768]{3,2,1,0:T(8,128)(2,1)S(1)}, bf16[2,2,128,768]{3,2,1,0:T(8,128)(2,1)S(1)}, u32[]{:S(2)}, u32[]{:S(2)}) collective-permute-start(bf16[2,2,128,768]{3,2,1,0:T(8,128)(2,1)S(1)} %dynamic-slice_bitcast_fusion.4), channel_id=1, source_target_pairs={{0,4},{1,5},{2,6},{3,7},{4,0},{5,1},{6,2},{7,3},{8,12},{9,13},{10,... | collective-permute-start | bytes 2359304 | tf_op jit(solution)/shard_map/ppermute | solution.py:191
  372.0 37.8 %collective-permute-start.66 = (bf16[2,2,2,32,1024]{4,3,2,1,0:T(8,128)(2,1)S(1)}, bf16[2,2,2,32,1024]{4,3,2,1,0:T(8,128)(2,1)S(1)}, u32[]{:S(2)}, u32[]{:S(2)}) collective-permute-start(bf16[2,2,2,32,1024]{4,3,2,1,0:T(8,128)(2,1)S(1)} %dynamic-slice_bitcast_fusion.8), channel_id=1, source_target_pairs={{0,16},{1,17},{2,18},{3,19},{4,20},{5,21},{6,22},{7,23},{8,24},{9,... | collective-permute-start | bytes 1572872 | tf_op jit(solution)/shard_map/ppermute | solution.py:191
  409.9 55.5 %collective-permute-start.55 = (bf16[2,128,768]{2,1,0:T(8,128)(2,1)S(1)}, bf16[2,128,768]{2,1,0:T(8,128)(2,1)S(1)}, u32[]{:S(2)}, u32[]{:S(2)}) collective-permute-start(bf16[2,128,768]{2,1,0:T(8,128)(2,1)S(1)} %dynamic-slice_bitcast_fusion.10), channel_id=1, source_target_pairs={{0,8},{1,9},{2,10},{3,11},{4,12},{5,13},{6,14},{7,15},{8,0},{9,1},... | collective-permute-start | bytes 1179656 | tf_op jit(solution)/shard_map/ppermute | solution.py:191
  430.3 28.8 %collective-permute-start.80 = (bf16[2,64,1024]{2,1,0:T(8,128)(2,1)S(1)}, bf16[2,64,1024]{2,1,0:T(8,128)(2,1)S(1)}, u32[]{:S(2)}, u32[]{:S(2)}) collective-permute-start(bf16[2,64,1024]{2,1,0:T(8,128)(2,1)S(1)} %dynamic-slice_bitcast_fusion.11), channel_id=1, source_target_pairs={{0,2},{1,3},{2,0},{3,1},{4,6},{5,7},{6,4},{7,5},{8,10},{9,11},{10,... | collective-permute-start | bytes 786440 | tf_op jit(solution)/shard_map/ppermute | solution.py:191
  433.5 31.1 %collective-permute-start.76 = (bf16[2,64,1024]{2,1,0:T(8,128)(2,1)S(1)}, bf16[2,64,1024]{2,1,0:T(8,128)(2,1)S(1)}, u32[]{:S(2)}, u32[]{:S(2)}) collective-permute-start(bf16[2,64,1024]{2,1,0:T(8,128)(2,1)S(1)} %dynamic-slice_bitcast_fusion.12), channel_id=1, source_target_pairs={{0,2},{1,3},{2,0},{3,1},{4,6},{5,7},{6,4},{7,5},{8,10},{9,11},{10,... | collective-permute-start | bytes 786440 | tf_op jit(solution)/shard_map/ppermute | solution.py:191
  434.8 48.2 %collective-permute-start.61 = (bf16[2,2,2,32,1024]{4,3,2,1,0:T(8,128)(2,1)}, bf16[2,2,2,32,1024]{4,3,2,1,0:T(8,128)(2,1)}, u32[]{:S(2)}, u32[]{:S(2)}) collective-permute-start(bf16[2,2,2,32,1024]{4,3,2,1,0:T(8,128)(2,1)} %dynamic-slice_bitcast_fusion.9), channel_id=1, source_target_pairs={{0,8},{1,9},{2,10},{3,11},{4,12},{5,13},{6,14},{7,15},{8,0},{9,1},... | collective-permute-start | bytes 1572872 | tf_op jit(solution)/shard_map/ppermute | solution.py:191
  (138 other events, 1879.6 us)

commit v2 on v1

--- a/solution.py
+++ b/solution.py
@@ -209,7 +209,7 @@
     return x
 
 
-def scatter(x, bits, left=()):
+def scatter(x, bits, left=(), last=F32):
     remaining = sorted(list(bits) + list(left), key=rank, reverse=True)
     for n, bit in enumerate(bits):
         place = remaining.index(bit)
@@ -218,13 +218,11 @@
         kept = lax.dynamic_index_in_dim(x, here, place, keepdims=False)
         x = kept.astype(F32) + swap(sent, bit).astype(F32)
         remaining.pop(place)
-        if n + 1 < len(bits):
-            x = x.astype(sent.dtype)
+        x = x.astype(sent.dtype if n + 1 < len(bits) else last)
     return x
 
 
-def unrelate(pieces):
-    me = lax.axis_index("ctx")
+def unrelate(pieces, me):
     for b in range(bits_of(len(pieces))):
         flip = ((me >> b) & 1) == 1
         pieces = [jnp.where(flip, pieces[j ^ (1 << b)], pieces[j]) for j in range(len(pieces))]
@@ -232,24 +230,90 @@
 
 
 def gather_ctx(x):
-    return unrelate([x] + [swap_by(x, 0, s) for s in range(1, lax.axis_size("ctx"))])
-
-
-def exchange_ctx(x):
+    others = [swap_by(x, 0, s) for s in range(1, lax.axis_size("ctx"))]
+    return unrelate([x] + others, lax.axis_index("ctx"))
+
+
+def exchange_ctx(pick):
     me = lax.axis_index("ctx")
-    pick = lambda j: lax.dynamic_index_in_dim(x, j, 0, keepdims=False)
-    return unrelate(
-        [pick(me)] + [swap_by(pick(me ^ s), 0, s) for s in range(1, lax.axis_size("ctx"))]
-    )
-
-
-def sum_ctx(x):
+    others = [swap_by(pick(me ^ s), 0, s) for s in range(1, lax.axis_size("ctx"))]
+    return unrelate([pick(me)] + others, me)
+
+
+def exchange_planes(pick):
+    me = lax.axis_index("dp") >> 1
+    others = [swap_by(pick(me ^ s), s << 1, 0) for s in range(1, lax.axis_size("dp") // 2)]
+    return unrelate([pick(me)] + others, me)
+
+
+def pool_rows(x, orders):
+    count = x.shape[0] // 2
+    halves = []
+    for part, bits in zip((x[:count], x[count:]), orders):
+        part = part[None]
+        for bit in bits:
+            part = jnp.concatenate([part, swap(part, bit)], 0)
+        halves.append(part)
+    return jnp.concatenate(halves, 0).reshape(-1, x.shape[1])
+
+
+def share_rows(x, orders):
+    planes = 2 ** len(orders[0])
+    x = x.reshape(2, planes, x.shape[0] // (2 * planes), x.shape[1])
+    halves = []
+    for part, bits in zip((x[0], x[1]), orders):
+        for bit in reversed(bits):
+            count = part.shape[0] // 2
+            other = swap(part[count:].astype(BF16), bit)
+            part = part[:count].astype(F32) + other.astype(F32)
+        halves.append(part[0])
+    return jnp.concatenate(halves, 0)
+
+
+def sum_ctx(pick):
     me = lax.axis_index("ctx")
-    pick = lambda j: lax.dynamic_index_in_dim(x, j, 0, keepdims=False)
     total = pick(me).astype(F32)
     for s in range(1, lax.axis_size("ctx")):
-        total = total + swap_by(pick(me ^ s).astype(BF16), 0, s).astype(F32)
+        total = total + swap_by(pick(me ^ s), 0, s).astype(F32)
     return total
+
+
+def send_ctx(x, steps):
+    ctx = lax.axis_size("ctx")
+    return lax.ppermute(
+        x, AXES, [(d * ctx + a, d * ctx + b) for d in range(lax.axis_size("dp")) for a, b in steps]
+    )
+
+
+def inner():
+    z = lax.axis_index("ctx")
+    return (z == 1) | (z == 2)
+
+
+def gather_line(x):
+    if lax.axis_size("ctx") != 4:
+        return gather(x, [("ctx", b) for b in range(bits_of(lax.axis_size("ctx")))])
+    pair = gather(x, [("ctx", 0)])
+    middle = send_ctx(pair, ((1, 2), (2, 1)))
+    outer = send_ctx(middle, ((1, 0), (2, 3)))
+    return join(pair, jnp.where(inner(), middle, outer), my_bit(("ctx", 1)), 0)
+
+
+def scatter_line(x):
+    if lax.axis_size("ctx") != 4:
+        return scatter(x, [("ctx", b) for b in range(bits_of(lax.axis_size("ctx")))][::-1])
+    side = my_bit(("ctx", 1))
+    far = lax.dynamic_index_in_dim(x, 1 - side, 0, keepdims=False)
+    near = lax.dynamic_index_in_dim(x, side, 0, keepdims=False)
+    passed = send_ctx(far, ((0, 1), (3, 2)))
+    far = (far.astype(F32) + passed.astype(F32)).astype(BF16)
+    crossed = send_ctx(far, ((1, 2), (2, 1)))
+    near = (near.astype(F32) + crossed.astype(F32)).astype(BF16)
+    return scatter(near, [("ctx", 0)])
+
+
+def after(x, *others):
+    return lax.optimization_barrier((x, *others))[0]
 
 
 def normalize(values):
@@ -297,8 +361,8 @@
     length = tokens * ctx
     width = HEADS * HD // ctx
     ff = b_up.shape[0] * devices
-    chunk = ff // 4
-    piece = b_up.shape[0] // 2
+    units = ff // planes
+    piece = b_up.shape[0]
     rows = d // devices
     core_bit = ("dp", 0)
     plane_bits = [("dp", b) for b in range(1, bits_of(dp))]
@@ -311,40 +375,48 @@
 
     small = [ln1_gain, ln1_bias, b_qv, b_out, ln2_gain, ln2_bias, b_up, b_down]
     sizes = [s.shape[0] for s in small]
-    packed = gather(jnp.concatenate(small)[None], ctx_bits + [core_bit] + plane_bits)
-    packed = packed.reshape(devices, sum(sizes))
+    placed = [
+        jnp.where(jnp.arange(size * ctx) // size == z, jnp.tile(v, ctx), 0)
+        for v, size in zip(small, sizes)
+    ]
+    share = sum(sizes) * ctx
+    extra = -(-share // (128 * rows)) * 128
+    placed = jnp.concatenate(placed + [jnp.zeros((rows * extra - share,), BF16)]).reshape(rows, extra)
+    by_head = w_qkv.reshape(rows, 3, ctx, width)
+    take = lambda j: jnp.concatenate(
+        [
+            lax.dynamic_index_in_dim(by_head, j, 2, keepdims=False).reshape(rows, 3 * width),
+            placed,
+            w_out,
+        ],
+        1,
+    )
+    own_cols = jnp.stack(exchange_ctx(take), 0)
+    wide = gather(own_cols, plane_bits + [core_bit])
+    wide = wide.reshape(dp, ctx, rows, 3 * width + extra + d)
+    proj_qkv = wide[..., : 3 * width].reshape(d, 3 * width)
+    proj_out = wide[..., 3 * width + extra :].reshape(d, d)
+    shares = wide[..., 3 * width : 3 * width + extra].astype(F32)
+    shares = jnp.sum(shares, axis=1).reshape(dp, rows * extra)
     whole = []
     start = 0
     for size in sizes:
-        whole.append(packed[:, start : start + size].reshape(devices * size).astype(F32))
-        start += size
+        whole.append(shares[:, start : start + size * ctx].reshape(devices * size))
+        start += size * ctx
     gain_first, shift_first, bias_qv, bias_out, gain_second, shift_second, bias_up, bias_down = whole
 
-    by_head = w_qkv.reshape(rows, 3, ctx, width).transpose(2, 0, 1, 3).reshape(ctx, rows, 3 * width)
-    own_cols = jnp.stack(exchange_ctx(by_head), 0)
-    proj_qkv = gather(own_cols, plane_bits + [core_bit]).reshape(d, 3 * width)
-
-    inputs_all = jnp.concatenate(gather_ctx(x_own), 0)
-
-    up_cols = w_up.reshape(rows, planes, 2, ctx, 2, piece)
-    up_pair = join(
-        lax.dynamic_index_in_dim(up_cols, core, 2, keepdims=False),
-        swap(lax.dynamic_index_in_dim(up_cols, 1 - core, 2, keepdims=False), core_bit),
-        core,
-        0,
-    )
+    inputs_all = jnp.concatenate(gather_ctx(after(x_own, own_cols)), 0)
+
     orders = (plane_bits, plane_bits[::-1])
-    proj_up, proj_down, bias_ups = [], [], []
-    bias_up_core = lax.dynamic_index_in_dim(
-        bias_up.reshape(planes, 2, ctx, 2, piece), core, 1, keepdims=False
-    )
-    for c in range(2):
-        part = up_pair[:, :, :, :, c].reshape(2, rows, planes * ctx * piece)
-        proj_up.append(gather(part, ctx_bits + orders[c], [core_bit]).reshape(d, chunk))
-        part = w_down[c * piece : (c + 1) * piece]
-        proj_down.append(gather(part, ctx_bits + orders[c]).reshape(chunk, d))
-        bias_ups.append(bias_up_core[:, :, c].reshape(chunk))
-    proj_out = gather(w_out, ctx_bits + plane_bits[::-1] + [core_bit]).reshape(d, d)
+    up_rows = jnp.stack(
+        exchange_planes(lambda p: lax.dynamic_slice_in_dim(w_up, p * units, units, 1)), 0
+    )
+    lines_up = gather_line(up_rows).reshape(ctx, planes, rows, units).transpose(1, 0, 2, 3)
+    proj_up = join(lines_up, swap(lines_up, core_bit), core, 1).reshape(d, units)
+    lines_down = gather_line(after(w_down, inputs_all))
+    proj_down = join(lines_down, swap(lines_down, core_bit), core, 0).reshape(units, d)
+    bias_up_own = lax.dynamic_slice_in_dim(bias_up, (lax.axis_index("dp") >> 1) * units, units, 0)
+    cot_pool = pool_rows(after(cot_own, wide), orders)
 
     hat_all, scale_all = normalize(inputs_all.astype(F32))
     hidden_first = (hat_all * gain_first + shift_first).astype(BF16)
@@ -353,48 +425,25 @@
     bias_mixed = jnp.concatenate([bias_heads[0], jnp.zeros((width,), F32), bias_heads[1]])
     mixed = (mixed + bias_mixed).astype(BF16)
     attended_heads, log_total = attention(prefix, mixed)
-    attended = jnp.concatenate(exchange_ctx(attended_heads.reshape(ctx, tokens, width)), 1)
+    attended = jnp.concatenate(
+        exchange_ctx(lambda j: lax.dynamic_slice_in_dim(attended_heads, j * tokens, tokens, 0)), 1
+    )
 
     inputs = x_own.astype(F32)
     resid = inputs + jnp.dot(attended, proj_out, preferred_element_type=F32) + bias_out
     hat_second, scale_second = normalize(resid)
     hidden_second = (hat_second * gain_second + shift_second).astype(BF16)
 
-    pair = lambda t: jnp.concatenate([t, swap(t, core_bit)], 0)
-    hidden_pair = pair(hidden_second)
-    cot_pair = pair(cot_own)
-    split_sum = lambda t: t[:tokens] + swap(t[tokens:].astype(BF16), core_bit).astype(F32)
-    out_part = 0.0
-    grad_hidden_part = 0.0
-    grads_down, grads_up, grads_bias_up = [], [], []
-    for c in range(2):
-        pre_act = (
-            jnp.dot(hidden_pair, proj_up[c], preferred_element_type=F32) + bias_ups[c]
-        )
-        gelu_value, gelu_pull = jax.vjp(gelu_tanh, pre_act)
-        activ = gelu_value.astype(BF16)
-        out_part += jnp.dot(activ, proj_down[c], preferred_element_type=F32)
-        grad_activ = dot_nt(cot_pair, proj_down[c])
-        grad_pre = gelu_pull(grad_activ)[0].astype(BF16)
-        grads_bias_up.append(jnp.sum(grad_pre.astype(F32), axis=0))
-        grad_hidden_part += dot_nt(grad_pre, proj_up[c])
-        grad = dot_tn(activ, cot_pair).astype(BF16)
-        grad = grad.reshape(twos(plane_bits) + twos(ctx_bits) + (piece, d))
-        grads_down.append(scatter(grad, orders[c] + ctx_bits[::-1]))
-        grad = dot_tn(hidden_pair, grad_pre).astype(BF16)
-        grad = grad.reshape(twos(plane_bits) + (2,) + twos(ctx_bits) + (rows, chunk))
-        grads_up.append(scatter(grad, orders[c] + ctx_bits[::-1], [core_bit]))
-    layer_out = (resid + split_sum(out_part) + bias_down).astype(BF16)
-    sum_down = jnp.concatenate(grads_down, 0)
-    up_sum = jnp.stack([g.reshape(2, rows, planes, ctx, piece) for g in grads_up], 4)
-    sum_up = join(
-        lax.dynamic_index_in_dim(up_sum, core, 0, keepdims=False),
-        swap(lax.dynamic_index_in_dim(up_sum, 1 - core, 0, keepdims=False).astype(BF16), core_bit).astype(F32),
-        core,
-        2,
-    ).reshape(rows, ff)
-
-    grad_hidden_second = split_sum(grad_hidden_part)
+    hidden_pool = pool_rows(hidden_second, orders)
+    pre_act = jnp.dot(hidden_pool, proj_up, preferred_element_type=F32) + bias_up_own
+    gelu_value, gelu_pull = jax.vjp(gelu_tanh, pre_act)
+    activ = gelu_value.astype(BF16)
+    grad_activ = dot_nt(cot_pool, proj_down)
+    grad_pre = gelu_pull(grad_activ)[0].astype(BF16)
+    grad_hidden_second = share_rows(dot_nt(grad_pre, proj_up), orders)
+    out_part = dot_nn(after(activ, grad_hidden_second), proj_down)
+    layer_out = (resid + share_rows(out_part, orders) + bias_down).astype(BF16)
+
     upstream = cot_own.astype(F32)
     grad_gain_second = jnp.sum(grad_hidden_second * hat_second, axis=0)
     grad_shift_second = jnp.sum(grad_hidden_second, axis=0)
@@ -403,39 +452,52 @@
     grad_bias_out = jnp.sum(grad_branch.astype(F32), axis=0)
     grad_attended = dot_nt(grad_branch, proj_out).astype(BF16)
     grad_heads = jnp.concatenate(
-        exchange_ctx(grad_attended.reshape(tokens, ctx, width).transpose(1, 0, 2)), 0
-    )
+        exchange_ctx(lambda j: lax.dynamic_slice_in_dim(grad_attended, j * width, width, 1)), 0
+    )
+
+    grad = dot_tn(activ, cot_pool).astype(BF16)
+    grad = grad.reshape((2,) + twos(ctx_bits) + (piece, d))
+    sum_down = scatter_line(scatter(grad, [core_bit], ctx_bits, BF16))
+    grad = dot_tn(hidden_pool, grad_pre).astype(BF16)
+    grad = grad.reshape(planes, 2, ctx, rows, units).transpose(1, 2, 0, 3, 4)
+    grad = grad.reshape((2,) + twos(ctx_bits) + (planes, rows, units))
+    up_sum = scatter_line(scatter(grad, [core_bit], ctx_bits, BF16)).astype(BF16)
+    columns = exchange_planes(lambda p: lax.dynamic_index_in_dim(up_sum, p, 0, keepdims=False))
+    sum_up = jnp.concatenate(columns, 1).astype(F32)
+
     grad_out = dot_tn(attended, grad_branch).astype(BF16)
     grad_out = grad_out.reshape(twos(plane_bits) + (2,) + twos(ctx_bits) + (rows, d))
-    sum_out = scatter(grad_out, [core_bit] + plane_bits + ctx_bits[::-1])
+    grad_out = scatter(grad_out, [core_bit] + plane_bits, ctx_bits, BF16)
+    sum_out = scatter_line(grad_out)
 
     grad_q, grad_k, grad_v = attention_grads(prefix, mixed, attended_heads, grad_heads, log_total)
     grad_mixed = jnp.concatenate([grad_q, grad_k, grad_v], 1)
     grad_hidden_all = dot_nt(grad_mixed, proj_qkv)
+    grad_gain_first = jnp.sum(grad_hidden_all * hat_all, axis=0)
+    grad_shift_first = jnp.sum(grad_hidden_all, axis=0)
+    grad_hidden_low = grad_hidden_all.astype(BF16)
+    grad_hidden_first = sum_ctx(
+        lambda j: lax.dynamic_slice_in_dim(grad_hidden_low, j * tokens, tokens, 0)
+    )
+    hat_first, scale_first = normalize(inputs)
+    input_grad = grad_resid + norm_back(grad_hidden_first, gain_first, hat_first, scale_first)
+
     grad_qkv = dot_tn(hidden_first, grad_mixed).astype(BF16)
     grad_qkv = grad_qkv.reshape((2,) * bits_of(dp) + (ctx * rows, 3 * width))
-    own_rows = scatter(grad_qkv, [core_bit] + plane_bits).astype(BF16)
-    columns = exchange_ctx(own_rows.reshape(ctx, rows, 3 * width))
+    own_rows = scatter(grad_qkv, [core_bit] + plane_bits, (), BF16).reshape(ctx, rows, 3 * width)
+    columns = exchange_ctx(lambda j: lax.dynamic_index_in_dim(own_rows, j, 0, keepdims=False))
     sum_qkv = (
         jnp.stack([c.reshape(rows, 3, width) for c in columns], 2)
         .reshape(rows, 3 * d)
         .astype(F32)
     )
 
-    grad_gain_first = jnp.sum(grad_hidden_all * hat_all, axis=0)
-    grad_shift_first = jnp.sum(grad_hidden_all, axis=0)
-    grad_hidden_first = sum_ctx(grad_hidden_all.reshape(ctx, tokens, d))
-    hat_first, scale_first = normalize(inputs)
-    input_grad = grad_resid + norm_back(grad_hidden_first, gain_first, hat_first, scale_first)
-
-    sums_heads = jnp.sum(grad_mixed.astype(F32), axis=0).reshape(3, 1, width)
-    at_heads = lambda t: lax.dynamic_update_slice(jnp.zeros((1, ctx, width), F32), t[None], (0, z, 0))
-    grad_bias_qv = jnp.concatenate([at_heads(sums_heads[0]), at_heads(sums_heads[2])], 0)
-    up_own = jnp.stack([g.reshape(planes, 1, ctx, piece) for g in grads_bias_up], 3)
-    grad_bias_up = lax.dynamic_update_slice(
-        jnp.zeros((planes, 2, ctx, 2, piece), F32), up_own, (0, core, 0, 0, 0)
-    )
-    grad_bias_down = jnp.sum(upstream, axis=0)
+    sums_heads = jnp.sum(grad_mixed.astype(F32), axis=0).reshape(3, width)
+    at_heads = lambda t: jnp.where(jnp.arange(d) // width == z, jnp.tile(t, ctx), 0)
+    grad_bias_qv = jnp.concatenate([at_heads(sums_heads[0]), at_heads(sums_heads[2])])
+    up_units = jnp.sum(grad_pre.astype(F32), axis=0)[None]
+    here = jnp.arange(planes)[:, None] == lax.axis_index("dp") >> 1
+    grad_bias_up = jnp.where(here, up_units, 0)
     grads = [
         grad_gain_first,
         grad_shift_first,
@@ -444,16 +506,17 @@
         grad_gain_second,
         grad_shift_second,
         grad_bias_up,
-        grad_bias_down,
+        jnp.sum(upstream, axis=0),
     ]
-    packed = jnp.concatenate([g.reshape(devices, size) for g, size in zip(grads, sizes)], 1)
-    packed = packed.reshape((2,) * bits_of(devices) + (1, sum(sizes)))
-    packed = scatter(packed, plane_bits + [core_bit] + ctx_bits)[0]
+    packed = jnp.concatenate([g.reshape(dp, size * ctx) for g, size in zip(grads, sizes)], 1)
+    packed = packed.reshape((2,) * bits_of(dp) + (share,))
+    packed = scatter(packed, plane_bits + [core_bit])
+    packed = packed + sum(swap_by(packed, 0, s) for s in range(1, ctx))
     sums = []
     start = 0
     for size in sizes:
-        sums.append(packed[start : start + size])
-        start += size
+        sums.append(lax.dynamic_slice_in_dim(packed, start + z * size, size, 0))
+        start += size * ctx
     (
         sum_gain_first,
         sum_shift_first,

time: 511 us -> 420 us (0.82)
  waiting for transfers between devices: 244 us -> 182 us
  local copies, waits for them, and re-layouts: 63.4 us -> 32.8 us
  starting transfers between devices: 90.1 us -> 107 us
  other arithmetic: 47.4 us -> 36.5 us
    ppermute x82 -> x64, waiting for transfers between devices: 244 us -> 149 us  [swap_by(): return lax.ppermute(x, AXES, pairs)]
    ppermute x0 -> x10, waiting for transfers between devices: none -> 33.4 us  [send_ctx(): lax.ppermute(x, AXES, [(d * ctx + a, d * ctx + b) for d in range(lax.axis...]
    concatenate x10 -> x5, local copies, waits for them, and re-layouts: 17.4 us -> 0.34 us  [the longest x1 0.25 us: per_device(): jnp.concatenate(placed + [jnp.zeros((rows * extra - share,), BF16)])]
    ppermute x0 -> x10, starting transfers between devices: none -> 13.8 us  [send_ctx(): lax.ppermute(x, AXES, [(d * ctx + a, d * ctx + b) for d in range(lax.axis...]
    squeeze x28 -> x11, local copies, waits for them, and re-layouts: 9.25 us -> 2.72 us  [scatter(): sent = lax.dynamic_index_in_dim(x, 1 - here, place, keepdims=False)]
    convert_element_type x22 -> x16, other arithmetic: 11 us -> 7.08 us  [the longest x8 4.35 us: scatter(): x = x.astype(sent.dtype if n + 1 < len(bits) else last)]
    ppermute x82 -> x64, starting transfers between devices: 90.1 us -> 93.6 us  [swap_by(): return lax.ppermute(x, AXES, pairs)]
    dot_general x6 -> x4, matrix products: 12.6 us -> 9.3 us  [dot_tn(): lax.dot_general(a, b, (((0,), (0,)), ((), ())), preferred_element_type=F32)]
  transfers between devices with their start and end apart: 82 -> 74, of which waited for: 38 -> 38; matrix products, arithmetic and copies ran while one was open for 26% -> 16% of each run, Pallas kernels for 3% -> 4%
where the time goes in v2:
time: 420 us; the launch traced here: 414 us
  waiting for transfers between devices  182 us (43%)
  starting transfers between devices  107 us (25%)
  other arithmetic  36.5 us (9%)
  matrix products  35 us (8%)
  local copies, waits for them, and re-layouts  32.8 us (8%)
  Pallas kernels  16.3 us (4%)
    ppermute x64, waiting for transfers between devices, swap_by(): return lax.ppermute(x, AXES, pairs)  149 us
    ppermute x64, starting transfers between devices, swap_by(): return lax.ppermute(x, AXES, pairs)  93.6 us
    ppermute x10, waiting for transfers between devices, send_ctx(): lax.ppermute(x, AXES, [(d * ctx + a, d * ctx + b) for d in range(lax.axis...  33.4 us
    dot_general x4, matrix products, dot_nt(): lax.dot_general(a, b, (((1,), (1,)), ((), ())), preferred_element_type=F32)  14.1 us
    ppermute x10, starting transfers between devices, send_ctx(): lax.ppermute(x, AXES, [(d * ctx + a, d * ctx + b) for d in range(lax.axis...  13.8 us
    another operation x18, other arithmetic, join(): jnp.stack([jnp.where(first, own, other), jnp.where(first, other, own)], a...  9.7 us
    dot_general x4, matrix products, dot_tn(): lax.dot_general(a, b, (((0,), (0,)), ((), ())), preferred_element_type=F32)  9.3 us
    pallas_call x1, Pallas kernels, attention_grads(): pl.pallas_call(functools.partial(attend_backward, rows=min(256, length)),...  8.95 us
  transfers between devices with their start and end apart: 74, of which 38 were waited for; matrix products, arithmetic and copies ran while one was open for 16% of the time, Pallas kernels for 4%

profile of v2, /device:TPU:0, one launch (start us, length us, event | category | flops | bytes accessed | tf_op | source)
XLA Modules:
  0.0 414.0 jit_solution(12336047858655695859)
XLA Ops:
  11.9 5.1 %collective-permute-start = (bf16[32,1920]{1,0:T(8,128)(2,1)S(1)}, bf16[32,1920]{1,0:T(8,128)(2,1)S(1)}, u32[]{:S(2)}, u32[]{:S(2)}) collective-permute-start(bf16[32,1920]{1,0:T(8,128)(2,1)S(1)} %get-tuple-element.148), channel_id=1, source_target_pairs={{0,3},{1,2},{2,1},{3,0},{4,7},{5,6},{6,5},{7,4},{8,11},{9,10},{10,... | collective-permute-start | bytes 368648 | tf_op jit(solution)/shard_map/ppermute | solution.py:191
  41.1 7.9 %collective-permute-done.3 = bf16[256,1024]{1,0:T(8,128)(2,1)S(1)} collective-permute-done((bf16[256,1024]{1,0:T(8,128)(2,1)S(1)}, bf16[256,1024]{1,0:T(8,128)(2,1)S(1)}, u32[]{:S(2)}, u32[]{:S(2)}) %collective-permute-start.3) | collective-permute-done | bytes 524320 | tf_op jit(solution)/shard_map/ppermute | solution.py:191
  49.0 30.5 %collective-permute-done.4 = bf16[256,1024]{1,0:T(8,128)(2,1)S(1)} collective-permute-done((bf16[256,1024]{1,0:T(8,128)(2,1)S(1)}, bf16[256,1024]{1,0:T(8,128)(2,1)S(1)}, u32[]{:S(2)}, u32[]{:S(2)}) %collective-permute-start.4) | collective-permute-done | bytes 524320 | tf_op jit(solution)/shard_map/ppermute | solution.py:191
  90.1 8.0 %collective-permute-done.21 = bf16[2,4,32,1024]{3,2,1,0:T(8,128)(2,1)} collective-permute-done((bf16[2,4,32,1024]{3,2,1,0:T(8,128)(2,1)}, bf16[2,4,32,1024]{3,2,1,0:T(8,128)(2,1)}, u32[]{:S(2)}, u32[]{:S(2)}) %collective-permute-start.21) | collective-permute-done | bytes 524320 | tf_op jit(solution)/shard_map/ppermute | solution.py:283
  103.3 12.4 %collective-permute-done.29 = bf16[2,128,1024]{2,1,0:T(8,128)(2,1)S(1)} collective-permute-done((bf16[2,128,1024]{2,1,0:T(8,128)(2,1)S(1)}, bf16[2,128,1024]{2,1,0:T(8,128)(2,1)S(1)}, u32[]{:S(2)}, u32[]{:S(2)}) %collective-permute-start.29) | collective-permute-done | bytes 524320 | tf_op jit(solution)/shard_map/ppermute | solution.py:283
  128.1 4.1 add_convert_fusion.q_ref.k_ref.v_ref
  132.3 7.3 %attend_forward.1 = (bf16[1024,256]{1,0:T(8,128)(2,1)S(1)}, f32[4,1,1024]{2,1,0:T(1,128)S(1)}) custom-call(s32[1]{0:T(128)S(6)} %copy.128.prefix_ref, bf16[1024,768]{1,0:T(8,128)(2,1)S(1)} %add_convert_fusion.q_ref.k_ref.v_ref, bf16[1024,768]{1,0:T(8,128)(2,1)S(1)} %add_convert_fusion.q_ref.k_ref.v_ref, bf16[1024,768]{1,0:T(8,128)(2,1)S(1)} %add_convert_fusion.q_ref.k_ref.v_ref), custom_call_target="tpu_custom_call" | custom-call | tf_op jit(solution)/shard_map/attend_forward/pallas_call | solution.py:134
  144.1 6.9 %collective-permute-done.10 = bf16[256,256]{1,0:T(8,128)(2,1)S(1)} collective-permute-done((bf16[256,256]{1,0:T(8,128)(2,1)S(1)}, bf16[256,256]{1,0:T(8,128)(2,1)S(1)}, u32[]{:S(2)}, u32[]{:S(2)}) %collective-permute-start.10) | collective-permute-done | bytes 131104 | tf_op jit(solution)/shard_map/ppermute | solution.py:191
  164.6 8.8 %collective-permute-done.24 = bf16[2,128,1024]{2,1,0:T(8,128)(2,1)S(1)} collective-permute-done((bf16[2,128,1024]{2,1,0:T(8,128)(2,1)S(1)}, bf16[2,128,1024]{2,1,0:T(8,128)(2,1)S(1)}, u32[]{:S(2)}, u32[]{:S(2)}) %collective-permute-start.24) | collective-permute-done | bytes 524320 | tf_op jit(solution)/shard_map/ppermute | solution.py:191
  173.7 9.1 %collective-permute-done.13 = bf16[2,128,1024]{2,1,0:T(8,128)(2,1)S(1)} collective-permute-done((bf16[2,128,1024]{2,1,0:T(8,128)(2,1)S(1)}, bf16[2,128,1024]{2,1,0:T(8,128)(2,1)S(1)}, u32[]{:S(2)}, u32[]{:S(2)}) %collective-permute-start.13) | collective-permute-done | bytes 524320 | tf_op jit(solution)/shard_map/ppermute | solution.py:191
  185.4 5.5 %convert_reduce_fusion.1 = (f32[1024]{0:T(1024)S(1)}, bf16[1024,1024]{1,0:T(8,128)(2,1)S(1)}, bf16[1024,1024]{1,0:T(8,128)(2,1)S(1)}) fusion(f32[1024,1024]{1,0:T(8,128)S(1)} %fusion.80, f32[1024]{0:T(1024)S(1)} %dynamic_slice.250, bf16[1024,1024]{1,0:T(8,128)(2,1)S(1)} %bitcast.351, bf16[1024,1024]{1,0:T(8,128)(2,1)S(1)} %bitcast.325), kind=kOutput, calls=%fused_computation.19 | convolution fusion | flops 2173697024 | bytes 12591104 | tf_op jit(solution)/shard_map/dot_general | solution.py:20
  195.9 4.4 %fusion.78 = (bf16[1024,1024]{1,0:T(8,128)(2,1)S(1)}, f32[1024,1024]{1,0:T(8,128)}) fusion(bf16[1024,1024]{1,0:T(8,128)(2,1)S(1)} %get-tuple-element.46, bf16[1024,1024]{1,0:T(8,128)(2,1)S(1)} %bitcast.328), kind=kOutput, calls=%fused_computation.363 | convolution fusion | flops 2148532224 | bytes 10485760 | tf_op jit(solution)/shard_map/dot_general | solution.py:20
  204.2 4.4 %fusion.79 = (bf16[1024,1024]{1,0:T(8,128)(2,1)S(1)}, f32[1024,1024]{1,0:T(8,128)}) fusion(bf16[1024,1024]{1,0:T(8,128)(2,1)S(1)} %get-tuple-element.27, bf16[1024,1024]{1,0:T(8,128)(2,1)S(1)} %bitcast.326), kind=kOutput, calls=%fused_computation.364 | convolution fusion | flops 2148532224 | bytes 10485760 | tf_op jit(solution)/shard_map/dot_general | solution.py:28
  217.7 6.9 %collective-permute-done.35 = bf16[2,128,1024]{2,1,0:T(8,128)(2,1)} collective-permute-done((bf16[2,128,1024]{2,1,0:T(8,128)(2,1)}, bf16[2,128,1024]{2,1,0:T(8,128)(2,1)}, u32[]{:S(2)}, u32[]{:S(2)}) %collective-permute-start.35) | collective-permute-done | bytes 524320 | tf_op jit(solution)/shard_map/ppermute | solution.py:191
  227.4 7.6 %collective-permute-done.31 = bf16[2,128,1024]{2,1,0:T(8,128)(2,1)} collective-permute-done((bf16[2,128,1024]{2,1,0:T(8,128)(2,1)}, bf16[2,128,1024]{2,1,0:T(8,128)(2,1)}, u32[]{:S(2)}, u32[]{:S(2)}) %collective-permute-start.31) | collective-permute-done | bytes 524320 | tf_op jit(solution)/shard_map/ppermute | solution.py:191
  241.5 6.5 %collective-permute-done.32 = bf16[1,128,1024]{2,1,0:T(8,128)(2,1)S(1)} collective-permute-done((bf16[1,128,1024]{2,1,0:T(8,128)(2,1)S(1)}, bf16[1,128,1024]{2,1,0:T(8,128)(2,1)S(1)}, u32[]{:S(2)}, u32[]{:S(2)}) %collective-permute-start.32) | collective-permute-done | bytes 262176 | tf_op jit(solution)/shard_map/ppermute | solution.py:191
  265.8 4.6 %collective-permute-done.40 = bf16[256,256]{1,0:T(8,128)(2,1)S(1)} collective-permute-done((bf16[256,256]{1,0:T(8,128)(2,1)S(1)}, bf16[256,256]{1,0:T(8,128)(2,1)S(1)}, u32[]{:S(2)}, u32[]{:S(2)}) %collective-permute-start.40) | collective-permute-done | bytes 131104 | tf_op jit(solution)/shard_map/ppermute | solution.py:191
  270.6 9.0 %attend_backward.1 = (bf16[1024,256]{1,0:T(8,128)(2,1)S(1)}, bf16[1024,256]{1,0:T(8,128)(2,1)S(1)}, bf16[1024,256]{1,0:T(8,128)(2,1)S(1)}) custom-call(s32[1]{0:T(128)S(6)} %copy.128.prefix_ref, bf16[1024,768]{1,0:T(8,128)(2,1)S(1)} %add_convert_fusion.q_ref.k_ref.v_ref, bf16[1024,768]{1,0:T(8,128)(2,1)S(1)} %add_convert_fusion.q_ref.k_ref.v_ref, ...), custom_call_target="tpu_custom_call" | custom-call | tf_op jit(solution)/shard_map/attend_backward/pallas_call | solution.py:156
  310.3 12.6 %collective-permute-done.42 = bf16[256,1024]{1,0:T(8,128)(2,1)S(1)} collective-permute-done((bf16[256,1024]{1,0:T(8,128)(2,1)S(1)}, bf16[256,1024]{1,0:T(8,128)(2,1)S(1)}, u32[]{:S(2)}, u32[]{:S(2)}) %collective-permute-start.42) | collective-permute-done | bytes 524320 | tf_op jit(solution)/shard_map/ppermute | solution.py:191
  324.6 16.4 %collective-permute-done.43 = bf16[256,1024]{1,0:T(8,128)(2,1)S(1)} collective-permute-done((bf16[256,1024]{1,0:T(8,128)(2,1)S(1)}, bf16[256,1024]{1,0:T(8,128)(2,1)S(1)}, u32[]{:S(2)}, u32[]{:S(2)}) %collective-permute-start.43) | collective-permute-done | bytes 524320 | tf_op jit(solution)/shard_map/ppermute | solution.py:191
  348.5 8.1 %collective-permute-done.64 = bf16[2,4,32,1024]{3,2,1,0:T(8,128)(2,1)S(1)} collective-permute-done((bf16[2,4,32,1024]{3,2,1,0:T(8,128)(2,1)S(1)}, bf16[2,4,32,1024]{3,2,1,0:T(8,128)(2,1)S(1)}, u32[]{:S(2)}, u32[]{:S(2)}) %collective-permute-start.64) | collective-permute-done | bytes 524320 | tf_op jit(solution)/shard_map/ppermute | solution.py:283
  361.4 8.6 %collective-permute-start.73 = (bf16[128,1024]{1,0:T(8,128)(2,1)}, bf16[128,1024]{1,0:T(8,128)(2,1)}, u32[]{:S(2)}, u32[]{:S(2)}) collective-permute-start(bf16[128,1024]{1,0:T(8,128)(2,1)} %dynamic-slice_bitcast_fusion.6), channel_id=1, source_target_pairs={{0,1},{1,0},{2,3},{3,2},{4,5},{5,4},{6,7},{7,6},{8,9},{9,8},{10,11... | collective-permute-start | bytes 786440 | tf_op jit(solution)/shard_map/ppermute | solution.py:191
  371.7 4.1 collective-permute-done.53
  402.0 8.6 %collective-permute-start.62 = (bf16[32,1024]{1,0:T(8,128)(2,1)S(1)}, bf16[32,1024]{1,0:T(8,128)(2,1)S(1)}, u32[]{:S(2)}, u32[]{:S(2)}) collective-permute-start(bf16[32,1024]{1,0:T(8,128)(2,1)S(1)} %dynamic-slice_bitcast_fusion.14), channel_id=1, source_target_pairs={{0,1},{1,0},{2,3},{3,2},{4,5},{5,4},{6,7},{7,6},{8,9},{9,8},{10,11... | collective-permute-start | bytes 196616 | tf_op jit(solution)/shard_map/ppermute | solution.py:191
  (473 shorter events, 202.7 us)
Async XLA Ops:
  32.3 16.8 %collective-permute-start.3 = (bf16[256,1024]{1,0:T(8,128)(2,1)S(1)}, bf16[256,1024]{1,0:T(8,128)(2,1)S(1)}, u32[]{:S(2)}, u32[]{:S(2)}) collective-permute-start(bf16[256,1024]{1,0:T(8,128)(2,1)S(1)} %bitcast.306), channel_id=1, source_target_pairs={{0,3},{1,2},{2,1},{3,0},{4,7},{5,6},{6,5},{7,4},{8,11},{9,10},{10,... | collective-permute-start | bytes 1572872 | tf_op jit(solution)/shard_map/ppermute | solution.py:191
  34.8 44.7 %collective-permute-start.4 = (bf16[256,1024]{1,0:T(8,128)(2,1)S(1)}, bf16[256,1024]{1,0:T(8,128)(2,1)S(1)}, u32[]{:S(2)}, u32[]{:S(2)}) collective-permute-start(bf16[256,1024]{1,0:T(8,128)(2,1)S(1)} %bitcast.307), channel_id=1, source_target_pairs={{0,2},{1,3},{2,0},{3,1},{4,6},{5,7},{6,4},{7,5},{8,10},{9,11},{10,... | collective-permute-start | bytes 1572872 | tf_op jit(solution)/shard_map/ppermute | solution.py:191
  34.8 44.7 %collective-permute-start.5 = (bf16[256,1024]{1,0:T(8,128)(2,1)S(1)}, bf16[256,1024]{1,0:T(8,128)(2,1)S(1)}, u32[]{:S(2)}, u32[]{:S(2)}) collective-permute-start(bf16[256,1024]{1,0:T(8,128)(2,1)S(1)} %bitcast.308), channel_id=1, source_target_pairs={{0,1},{1,0},{2,3},{3,2},{4,5},{5,4},{6,7},{7,6},{8,9},{9,8},{10,11... | collective-permute-start | bytes 1572872 | tf_op jit(solution)/shard_map/ppermute | solution.py:191
  36.9 45.9 %collective-permute-start.20 = (bf16[2,4,32,1024]{3,2,1,0:T(8,128)(2,1)S(1)}, bf16[2,4,32,1024]{3,2,1,0:T(8,128)(2,1)}, u32[]{:S(2)}, u32[]{:S(2)}) collective-permute-start(bf16[2,4,32,1024]{3,2,1,0:T(8,128)(2,1)S(1)} %pad_maximum_fusion.12), channel_id=1, source_target_pairs={{1,2},{2,1},{5,6},{6,5},{9,10},{10,9},{13,14},{14,13},{17,18},{18,... | collective-permute-start | bytes 1572872 | tf_op jit(solution)/shard_map/ppermute | solution.py:283
  81.4 19.8 %collective-permute-start.7 = (bf16[2,4,32,1920]{3,2,1,0:T(8,128)(2,1)}, bf16[2,4,32,1920]{3,2,1,0:T(8,128)(2,1)}, u32[]{:S(2)}, u32[]{:S(2)}) collective-permute-start(bf16[2,4,32,1920]{3,2,1,0:T(8,128)(2,1)} %pad_maximum_fusion.8), channel_id=1, source_target_pairs={{0,16},{1,17},{2,18},{3,19},{4,20},{5,21},{6,22},{7,23},{8,24},{9,... | collective-permute-start | bytes 2949128 | tf_op jit(solution)/shard_map/ppermute | solution.py:191
  99.5 17.3 %collective-permute-start.22 = (bf16[4,4,32,1024]{3,2,1,0:T(8,128)(2,1)S(1)}, bf16[4,4,32,1024]{3,2,1,0:T(8,128)(2,1)S(1)}, u32[]{:S(2)}, u32[]{:S(2)}) collective-permute-start(bf16[4,4,32,1024]{3,2,1,0:T(8,128)(2,1)S(1)} %bitcast.316), channel_id=1, source_target_pairs={{0,4},{1,5},{2,6},{3,7},{4,0},{5,1},{6,2},{7,3},{8,12},{9,13},{10,... | collective-permute-start | bytes 3145736 | tf_op jit(solution)/shard_map/ppermute | solution.py:191
  102.8 17.6 %collective-permute-start.8 = (bf16[2,2,4,32,1920]{4,3,2,1,0:T(8,128)(2,1)S(1)}, bf16[2,2,4,32,1920]{4,3,2,1,0:T(8,128)(2,1)S(1)}, u32[]{:S(2)}, u32[]{:S(2)}) collective-permute-start(bf16[2,2,4,32,1920]{4,3,2,1,0:T(8,128)(2,1)S(1)} %pad_maximum_fusion.4), channel_id=1, source_target_pairs={{0,4},{1,5},{2,6},{3,7},{4,0},{5,1},{6,2},{7,3},{8,12},{9,13},{10,... | collective-permute-start | bytes 5898248 | tf_op jit(solution)/shard_map/ppermute | solution.py:191
  125.7 29.4 %collective-permute-start.23 = (bf16[1,128,1024]{2,1,0:T(8,128)(2,1)}, bf16[1,128,1024]{2,1,0:T(8,128)(2,1)}, u32[]{:S(2)}, u32[]{:S(2)}) collective-permute-start(bf16[1,128,1024]{2,1,0:T(8,128)(2,1)} %get-tuple-element.105), channel_id=1, source_target_pairs={{0,8},{1,9},{2,10},{3,11},{4,12},{5,13},{6,14},{7,15},{8,0},{9,1},... | collective-permute-start | bytes 786440 | tf_op jit(solution)/shard_map/ppermute | solution.py:191
  126.2 31.5 %collective-permute-start.25 = (bf16[1,128,1024]{2,1,0:T(8,128)(2,1)}, bf16[1,128,1024]{2,1,0:T(8,128)(2,1)S(1)}, u32[]{:S(2)}, u32[]{:S(2)}) collective-permute-start(bf16[1,128,1024]{2,1,0:T(8,128)(2,1)} %get-tuple-element.104), channel_id=1, source_target_pairs={{0,16},{1,17},{2,18},{3,19},{4,20},{5,21},{6,22},{7,23},{8,24},{9,... | collective-permute-start | bytes 786440 | tf_op jit(solution)/shard_map/ppermute | solution.py:191
  156.2 17.2 %collective-permute-start.24 = (bf16[2,128,1024]{2,1,0:T(8,128)(2,1)S(1)}, bf16[2,128,1024]{2,1,0:T(8,128)(2,1)S(1)}, u32[]{:S(2)}, u32[]{:S(2)}) collective-permute-start(bf16[2,128,1024]{2,1,0:T(8,128)(2,1)S(1)} %pad_maximum_fusion.13), channel_id=1, source_target_pairs={{0,16},{1,17},{2,18},{3,19},{4,20},{5,21},{6,22},{7,23},{8,24},{9,... | collective-permute-start | bytes 1572872 | tf_op jit(solution)/shard_map/ppermute | solution.py:191
  162.2 20.8 %collective-permute-start.15 = (bf16[2,128,1024]{2,1,0:T(8,128)(2,1)S(1)}, bf16[2,128,1024]{2,1,0:T(8,128)(2,1)S(1)}, u32[]{:S(2)}, u32[]{:S(2)}) collective-permute-start(bf16[2,128,1024]{2,1,0:T(8,128)(2,1)S(1)} %pad_maximum_fusion.11), channel_id=1, source_target_pairs={{0,8},{1,9},{2,10},{3,11},{4,12},{5,13},{6,14},{7,15},{8,0},{9,1},... | collective-permute-start | bytes 1572872 | tf_op jit(solution)/shard_map/ppermute | solution.py:191
  163.9 18.9 %collective-permute-start.13 = (bf16[2,128,1024]{2,1,0:T(8,128)(2,1)S(1)}, bf16[2,128,1024]{2,1,0:T(8,128)(2,1)S(1)}, u32[]{:S(2)}, u32[]{:S(2)}) collective-permute-start(bf16[2,128,1024]{2,1,0:T(8,128)(2,1)S(1)} %pad_maximum_fusion.10), channel_id=1, source_target_pairs={{0,16},{1,17},{2,18},{3,19},{4,20},{5,21},{6,22},{7,23},{8,24},{9,... | collective-permute-start | bytes 1572872 | tf_op jit(solution)/shard_map/ppermute | solution.py:191
  201.3 103.2 %collective-permute-start.70 = (bf16[2,2,128,1024]{3,2,1,0:T(8,128)(2,1)}, bf16[2,2,128,1024]{3,2,1,0:T(8,128)(2,1)}, u32[]{:S(2)}, u32[]{:S(2)}) collective-permute-start(bf16[2,2,128,1024]{3,2,1,0:T(8,128)(2,1)} %dynamic-slice_bitcast_fusion), channel_id=1, source_target_pairs={{0,4},{1,5},{2,6},{3,7},{4,0},{5,1},{6,2},{7,3},{8,12},{9,13},{10,... | collective-permute-start | bytes 3145736 | tf_op jit(solution)/shard_map/ppermute | solution.py:191
  203.7 104.7 %collective-permute-start.63 = (bf16[2,2,4,32,1024]{4,3,2,1,0:T(8,128)(2,1)}, bf16[2,2,4,32,1024]{4,3,2,1,0:T(8,128)(2,1)}, u32[]{:S(2)}, u32[]{:S(2)}) collective-permute-start(bf16[2,2,4,32,1024]{4,3,2,1,0:T(8,128)(2,1)} %bitcast.300), channel_id=1, source_target_pairs={{0,4},{1,5},{2,6},{3,7},{4,0},{5,1},{6,2},{7,3},{8,12},{9,13},{10,... | collective-permute-start | bytes 3145736 | tf_op jit(solution)/shard_map/ppermute | solution.py:191
  211.1 27.4 %collective-permute-start.37 = (bf16[2,128,1024]{2,1,0:T(8,128)(2,1)}, bf16[2,128,1024]{2,1,0:T(8,128)(2,1)}, u32[]{:S(2)}, u32[]{:S(2)}) collective-permute-start(bf16[2,128,1024]{2,1,0:T(8,128)(2,1)} %bitcast.63), channel_id=1, source_target_pairs={{0,8},{1,9},{2,10},{3,11},{4,12},{5,13},{6,14},{7,15},{8,0},{9,1},... | collective-permute-start | bytes 1572872 | tf_op jit(solution)/shard_map/ppermute | solution.py:191
  213.6 21.4 %collective-permute-start.31 = (bf16[2,128,1024]{2,1,0:T(8,128)(2,1)}, bf16[2,128,1024]{2,1,0:T(8,128)(2,1)}, u32[]{:S(2)}, u32[]{:S(2)}) collective-permute-start(bf16[2,128,1024]{2,1,0:T(8,128)(2,1)} %bitcast.54), channel_id=1, source_target_pairs={{0,16},{1,17},{2,18},{3,19},{4,20},{5,21},{6,22},{7,23},{8,24},{9,... | collective-permute-start | bytes 1572872 | tf_op jit(solution)/shard_map/ppermute | solution.py:191
  299.4 60.0 %collective-permute-start.57 = (bf16[2,2,2,2,32,1024]{5,4,3,2,0,1:T(8,128)(2,1)S(1)}, bf16[2,2,2,2,32,1024]{5,4,3,2,0,1:T(8,128)(2,1)S(1)}, u32[]{:S(2)}, u32[]{:S(2)}) collective-permute-start(bf16[2,2,2,2,32,1024]{5,4,3,2,0,1:T(8,128)(2,1)S(1)} %bitcast.333), channel_id=1, source_target_pairs={{0,4},{1,5},{2,6},{3,7},{4,0},{5,1},{6,2},{7,3},{8,12},{9,13},{10,... | collective-permute-start | bytes 3145736 | tf_op jit(solution)/shard_map/ppermute | solution.py:191
  299.5 23.4 %collective-permute-start.42 = (bf16[256,1024]{1,0:T(8,128)(2,1)S(1)}, bf16[256,1024]{1,0:T(8,128)(2,1)S(1)}, u32[]{:S(2)}, u32[]{:S(2)}) collective-permute-start(bf16[256,1024]{1,0:T(8,128)(2,1)S(1)} %get-tuple-element.64), channel_id=1, source_target_pairs={{0,1},{1,0},{2,3},{3,2},{4,5},{5,4},{6,7},{7,6},{8,9},{9,8},{10,11... | collective-permute-start | bytes 1572872 | tf_op jit(solution)/shard_map/ppermute | solution.py:191
  302.7 38.2 %collective-permute-start.43 = (bf16[256,1024]{1,0:T(8,128)(2,1)S(1)}, bf16[256,1024]{1,0:T(8,128)(2,1)S(1)}, u32[]{:S(2)}, u32[]{:S(2)}) collective-permute-start(bf16[256,1024]{1,0:T(8,128)(2,1)S(1)} %get-tuple-element.66), channel_id=1, source_target_pairs={{0,2},{1,3},{2,0},{3,1},{4,6},{5,7},{6,4},{7,5},{8,10},{9,11},{10,... | collective-permute-start | bytes 1572872 | tf_op jit(solution)/shard_map/ppermute | solution.py:191
  304.5 37.8 %collective-permute-start.44 = (bf16[256,1024]{1,0:T(8,128)(2,1)S(1)}, bf16[256,1024]{1,0:T(8,128)(2,1)S(1)}, u32[]{:S(2)}, u32[]{:S(2)}) collective-permute-start(bf16[256,1024]{1,0:T(8,128)(2,1)S(1)} %get-tuple-element.65), channel_id=1, source_target_pairs={{0,3},{1,2},{2,1},{3,0},{4,7},{5,6},{6,5},{7,4},{8,11},{9,10},{10,... | collective-permute-start | bytes 1572872 | tf_op jit(solution)/shard_map/ppermute | solution.py:191
  308.4 49.2 %collective-permute-start.51 = (bf16[2,2,128,768]{3,2,1,0:T(8,128)(2,1)S(1)}, bf16[2,2,128,768]{3,2,1,0:T(8,128)(2,1)S(1)}, u32[]{:S(2)}, u32[]{:S(2)}) collective-permute-start(bf16[2,2,128,768]{3,2,1,0:T(8,128)(2,1)S(1)} %dynamic-slice_bitcast_fusion.1), channel_id=1, source_target_pairs={{0,4},{1,5},{2,6},{3,7},{4,0},{5,1},{6,2},{7,3},{8,12},{9,13},{10,... | collective-permute-start | bytes 2359304 | tf_op jit(solution)/shard_map/ppermute | solution.py:191
  322.8 24.8 %collective-permute-start.71 = (bf16[2,128,1024]{2,1,0:T(8,128)(2,1)S(1)}, bf16[2,128,1024]{2,1,0:T(8,128)(2,1)S(1)}, u32[]{:S(2)}, u32[]{:S(2)}) collective-permute-start(bf16[2,128,1024]{2,1,0:T(8,128)(2,1)S(1)} %dynamic-slice_bitcast_fusion.2), channel_id=1, source_target_pairs={{0,1},{3,2},{4,5},{7,6},{8,9},{11,10},{12,13},{15,14},{16,17},{19,... | collective-permute-start | bytes 1572872 | tf_op jit(solution)/shard_map/ppermute | solution.py:283
  359.9 27.6 %collective-permute-start.58 = (bf16[2,2,2,32,1024]{4,3,2,1,0:T(8,128)(2,1)S(1)}, bf16[2,2,2,32,1024]{4,3,2,1,0:T(8,128)(2,1)S(1)}, u32[]{:S(2)}, u32[]{:S(2)}) collective-permute-start(bf16[2,2,2,32,1024]{4,3,2,1,0:T(8,128)(2,1)S(1)} %dynamic-slice_bitcast_fusion.4), channel_id=1, source_target_pairs={{0,8},{1,9},{2,10},{3,11},{4,12},{5,13},{6,14},{7,15},{8,0},{9,1},... | collective-permute-start | bytes 1572872 | tf_op jit(solution)/shard_map/ppermute | solution.py:191
  361.4 36.6 %collective-permute-start.73 = (bf16[128,1024]{1,0:T(8,128)(2,1)}, bf16[128,1024]{1,0:T(8,128)(2,1)}, u32[]{:S(2)}, u32[]{:S(2)}) collective-permute-start(bf16[128,1024]{1,0:T(8,128)(2,1)} %dynamic-slice_bitcast_fusion.6), channel_id=1, source_target_pairs={{0,1},{1,0},{2,3},{3,2},{4,5},{5,4},{6,7},{7,6},{8,9},{9,8},{10,11... | collective-permute-start | bytes 786440 | tf_op jit(solution)/shard_map/ppermute | solution.py:191
  (110 other events, 1079.4 us)
